TPU v7x, 512 devices: a whole 4x8x8 slice. The times are simulated.
512 devices in a mesh: tensor: 8 (over x, core), context: 64 (over z, y).
Axes of the slice: x: 4, y: 8, z: 8, core: 2. Of those that a mesh axis runs over, the one named last changes fastest.
Arguments:
- token_ids: int32 [2, 6144], P(None, 'context'), may hold values from 0 to 151935
- embed_table: bfloat16 [4096, 151936], P('context', 'tensor')
- input_gain: float32 [4096], replicated, may hold values from 0.1 to 1.9
- w_qkv: bfloat16 [4096, 6144], P('context', 'tensor')
- q_gain: float32 [128], replicated, may hold values from 1 to 10
- k_gain: float32 [128], replicated, may hold values from 1 to 10
Outputs:
- attended: bfloat16 [64, 6144, 128], P('context', 'tensor')
All inputs are finite; a program needn't handle non-finite values.
Results may differ from a plain program's by a relative error of at most 0.0085.
The roundings to bfloat16 on the way count: a program that leaves them out, or rounds other values in their place, can miss the bound.
Values may be sent and summed in bfloat16 or wider, within the bound.
A program may use at most 64 MiB of HBM per device.

v0:
```python
import math

import jax
import jax.numpy as jnp
from jax import lax
from jax.sharding import PartitionSpec as P

QH = 32
KVH = 8
HD = 128


ROPE_BASE = 1000000.0
EPSILON = 1e-06
NEGATIVE = -1e30


def rope_tables(positions, width):
    half_width = width // 2
    exponent = jnp.arange(half_width, dtype=jnp.float32) * (2.0 / width)
    inverse = jnp.exp(-exponent * jnp.log(jnp.float32(ROPE_BASE)))
    angles = positions.astype(jnp.float32)[:, None] * inverse[None, :]
    angles = jnp.concatenate([angles, angles], axis=-1)
    return (jnp.cos(angles), jnp.sin(angles))


def norm_rope(head_vals, head_gain, cos_table, sin_table):
    mean_sq = jnp.mean(head_vals * head_vals, axis=-1, keepdims=True)
    scaled = head_vals * lax.rsqrt(mean_sq + EPSILON) * head_gain
    half_width = scaled.shape[-1] // 2
    rotated = jnp.concatenate([-scaled[..., half_width:], scaled[..., :half_width]], axis=-1)
    return scaled * cos_table[:, None, :] + rotated * sin_table[:, None, :]


def feature_norm(embedded, input_gain):
    hidden = embedded.astype(jnp.float32)
    mean_sq = jnp.mean(hidden * hidden, axis=0, keepdims=True)
    return (hidden * lax.rsqrt(mean_sq + EPSILON) * input_gain[:, None, None]).astype(jnp.bfloat16)


def shards(token_ids, embed_table, input_gain, w_qkv, q_gain, k_gain):
    tensor_count = lax.axis_size("tensor")
    tensor_rank = lax.axis_index("tensor")
    context_rank = lax.axis_index("context")
    seq_count, local_len = token_ids.shape
    width_part, vocab_part = embed_table.shape
    all_ids = lax.all_gather(token_ids, "context", axis=1, tiled=True)
    full_len = all_ids.shape[1]
    local_ids = all_ids - tensor_rank * vocab_part
    inside = (local_ids >= 0) & (local_ids < vocab_part)
    picked = jnp.take(embed_table, jnp.clip(local_ids, 0, vocab_part - 1), axis=1)
    partial_rows = jnp.where(inside[None], picked.astype(jnp.float32), 0.0)
    summed = lax.psum(partial_rows.astype(jnp.bfloat16), "tensor")
    embedded = lax.all_to_all(summed, "context", split_axis=2, concat_axis=0, tiled=True)
    normed = feature_norm(embedded, input_gain)
    projected = jnp.einsum(
        "dsl,dk->slk",
        normed,
        lax.all_gather(w_qkv, "context", axis=0, tiled=True),
        preferred_element_type=jnp.float32,
    )
    joined_proj = lax.all_gather(projected.astype(jnp.bfloat16), "tensor", axis=2, tiled=True)
    positions = context_rank * local_len + jnp.arange(local_len, dtype=jnp.int32)
    cos_table, sin_table = rope_tables(positions, HD)
    wide = joined_proj.astype(jnp.float32)
    queries = norm_rope(
        wide[..., : QH * HD].reshape(seq_count, local_len, QH, HD), q_gain, cos_table, sin_table
    ).astype(jnp.bfloat16)
    key_heads = norm_rope(
        wide[..., QH * HD : (QH + KVH) * HD].reshape(seq_count, local_len, KVH, HD),
        k_gain,
        cos_table,
        sin_table,
    ).astype(jnp.bfloat16)
    values = joined_proj[..., (QH + KVH) * HD :].reshape(seq_count, local_len, KVH, HD)
    group_size = QH // KVH
    queries = jnp.transpose(queries, (0, 2, 1, 3)).reshape(seq_count * QH, local_len, HD)
    key_heads = jnp.repeat(jnp.transpose(key_heads, (0, 2, 1, 3)), group_size, axis=1).reshape(
        seq_count * QH, local_len, HD
    )
    values = jnp.repeat(jnp.transpose(values, (0, 2, 1, 3)), group_size, axis=1).reshape(
        seq_count * QH, local_len, HD
    )
    queries, key_heads, values = (
        lax.all_to_all(queries, "context", split_axis=0, concat_axis=1, tiled=True),
        lax.all_to_all(key_heads, "context", split_axis=0, concat_axis=1, tiled=True),
        lax.all_to_all(values, "context", split_axis=0, concat_axis=1, tiled=True),
    )
    unit_count = queries.shape[0]
    block_rows = full_len // tensor_count
    own_queries = lax.dynamic_slice_in_dim(queries, tensor_rank * block_rows, block_rows, 1)
    query_pos = tensor_rank * block_rows + jnp.arange(block_rows, dtype=jnp.int32)
    query_block = math.gcd(block_rows, 512)
    query_steps = block_rows // query_block
    key_block = math.gcd(full_len, 512)
    key_steps = full_len // key_block
    key_tiles = key_heads.reshape(unit_count, key_steps, key_block, HD)
    value_tiles = values.reshape(unit_count, key_steps, key_block, HD)
    score_scale = HD ** (-0.5)
    outputs = []
    for q_index in range(query_steps):
        query_tile = own_queries[:, q_index * query_block : (q_index + 1) * query_block]
        block_pos = query_pos[q_index * query_block : (q_index + 1) * query_block]
        last_pos = jnp.max(block_pos)

        def key_step(key_index, state_now):
            key_start = key_index * key_block

            def attend(state_in):
                old_max, old_total, old_acc = state_in
                key_tile = lax.dynamic_index_in_dim(key_tiles, key_index, 1, keepdims=False)
                value_tile = lax.dynamic_index_in_dim(value_tiles, key_index, 1, keepdims=False)
                scores = (
                    jnp.einsum(
                        "uqd,ukd->uqk", query_tile, key_tile, preferred_element_type=jnp.float32
                    )
                    * score_scale
                )
                key_pos = key_start + jnp.arange(key_block, dtype=jnp.int32)
                allowed = (key_pos[None, :] <= block_pos[:, None])[None]
                scores = jnp.where(allowed, scores, NEGATIVE)
                new_max = jnp.maximum(old_max, jnp.max(scores, axis=-1))
                weights = jnp.where(allowed, jnp.exp(scores - new_max[..., None]), 0.0)
                shrink = jnp.exp(old_max - new_max)
                new_total = old_total * shrink + jnp.sum(weights, axis=-1)
                new_acc = old_acc * shrink[..., None] + jnp.einsum(
                    "uqk,ukd->uqd",
                    weights.astype(jnp.bfloat16),
                    value_tile,
                    preferred_element_type=jnp.float32,
                )
                return (new_max, new_total, new_acc)

            return lax.cond(key_start <= last_pos, attend, lambda unchanged: unchanged, state_now)

        starting = (
            jnp.full((unit_count, query_block), NEGATIVE, jnp.float32),
            jnp.zeros((unit_count, query_block), jnp.float32),
            jnp.zeros((unit_count, query_block, HD), jnp.float32),
        )
        run_max, run_total, run_acc = lax.fori_loop(0, key_steps, key_step, starting)
        outputs.append((run_acc / run_total[..., None]).astype(jnp.bfloat16))
    attended = jnp.concatenate(outputs, axis=1)
    return attended


def solution(mesh):
    return jax.shard_map(
        shards,
        mesh=mesh,
        in_specs=(
            P(None, "context"),
            P("context", "tensor"),
            P(),
            P("context", "tensor"),
            P(),
            P(),
        ),
        out_specs=P("context", "tensor", None),
        check_vma=False,
    )
```

profile of v0, /device:TPU:15, one launch (start us, length us, event | category | flops | bytes accessed | tf_op | source)
XLA Modules:
  0.0 587.7 jit_solution(8688220472509900719)
XLA Ops:
  7.4 43.1 %all-gather = s32[64,96,2]{1,2,0:T(2,128)S(1)} all-gather(s32[1,96,2]{1,2,0:T(2,128)} %bitcast.203), channel_id=1, replica_groups=mesh['tensor'=8,'context'=64] {'context'}, dimensions={0}, use_global_device_ids=true | all-gather | bytes 49920 | tf_op jit(solution)/shard_map/all_gather | solution.py:47
  50.8 5.8 copy.85
  60.4 35.7 %gather_fusion = bf16[12288,64]{1,0:T(8,128)(2,1)S(1)} fusion(bf16[64,18992]{0,1:T(8,128)(2,1)} %copy.85, s32[12288]{0:T(1024)S(1)} %broadcast_clamp_fusion), kind=kCustom, calls=%fused_computation | custom fusion | bytes 3194880 | tf_op jit(solution)/shard_map/jit(_take)/gather | solution.py:51
  96.1 29.7 %fusion.58 = bf16[64,2,6144]{0,1,2:T(2,128)(2,1)} fusion(pred[2,6144]{0,1:T(8,128)(4,1)} %copy.84, pred[2,6144]{0,1:T(8,128)(4,1)} %copy.83, bf16[2,6144,64]{2,1,0:T(8,128)(2,1)S(1)} %bitcast.176), kind=kLoop, calls=%fused_computation.77 | loop fusion | flops 3145728 | bytes 3170304 | tf_op jit(solution)/shard_map/convert_element_type | solution.py:53
  126.3 89.2 %all-reduce.2.cloned.1.call-done = bf16[64,2,6144]{0,1,2:T(2,128)(2,1)} async-done(((bf16[64,2,6144]{0,1,2:T(2,128)(2,1)}), bf16[64,2,6144]{0,1,2:T(2,128)(2,1)}) %all-reduce.2.cloned.1.call-update) | async-done | bytes 1572880 | tf_op jit(solution)/shard_map/psum | solution.py:53
  215.6 7.8 %reshape.275 = bf16[64,2,6144]{2,1,0:T(2,128)(2,1)} reshape(bf16[6144,2,64]{2,1,0:T(2,128)(2,1)} %bitcast.179) | data formatting | bytes 3145728
  223.4 12.8 %all-to-all-start = ((bf16[64,2,6144]{2,1,0:T(2,128)(2,1)}), bf16[64,2,6144]{2,1,0:T(2,128)(2,1)S(1)}, u32[]{:S(2)}, u32[]{:S(2)}) async-start(bf16[64,2,6144]{2,1,0:T(2,128)(2,1)} %reshape.275), calls=%async_computation | async-start | bytes 3145728 | tf_op jit(solution)/shard_map/all_to_all | solution.py:54
  236.4 40.8 %all-to-all-done = bf16[64,2,6144]{2,1,0:T(2,128)(2,1)S(1)} async-done(((bf16[64,2,6144]{2,1,0:T(2,128)(2,1)}), bf16[64,2,6144]{2,1,0:T(2,128)(2,1)S(1)}, u32[]{:S(2)}, u32[]{:S(2)}) %all-to-all-start) | async-done | bytes 1572896 | tf_op jit(solution)/shard_map/all_to_all | solution.py:54
  277.3 3.4 reshape.276
  280.7 6.3 %copy.87 = bf16[64,2,6144]{2,0,1:T(8,128)(2,1)S(1)} copy(bf16[64,2,6144]{0,1,2:T(2,128)(2,1)} %bitcast.169) | data formatting | bytes 3145728 | tf_op jit(solution)/shard_map/all_to_all | solution.py:54
  286.9 3.2 reshape.251
  290.2 6.7 %copy.88 = f32[64,64,2,96]{3,1,0,2:T(8,128)} copy(f32[64,64,2,96]{3,0,1,2:T(8,128)} %bitcast.168) | data formatting | bytes 6291456 | tf_op jit(solution)/shard_map/convert_element_type | solution.py:36
  298.7 2.6 fusion.57
  301.3 4.9 fusion.63
  306.6 26.0 %all-gather.6.cloned.1.call-done = bf16[2,96,6144]{2,1,0:T(8,128)(2,1)} async-done(((bf16[2,96,768]{2,1,0:T(8,128)(2,1)}), bf16[2,96,6144]{2,1,0:T(8,128)(2,1)}) %all-gather.6.cloned.1.call-update) | async-done | bytes 2359312 | tf_op jit(solution)/shard_map/all_gather | solution.py:62
  339.5 3.0 fusion.62
  342.5 13.1 %all-to-all-start.2 = ((bf16[64,96,128]{2,1,0:T(8,128)(2,1)}), bf16[64,96,128]{2,1,0:T(8,128)(2,1)}, u32[]{:S(2)}, u32[]{:S(2)}) async-start(bf16[64,96,128]{2,1,0:T(8,128)(2,1)} %bitcast.178), calls=%async_computation.2 | async-start | bytes 3145728 | tf_op jit(solution)/shard_map/all_to_all | solution.py:85
  357.4 38.0 %all-to-all-done.2 = bf16[64,96,128]{2,1,0:T(8,128)(2,1)} async-done(((bf16[64,96,128]{2,1,0:T(8,128)(2,1)}), bf16[64,96,128]{2,1,0:T(8,128)(2,1)}, u32[]{:S(2)}, u32[]{:S(2)}) %all-to-all-start.2) | async-done | bytes 1572896 | tf_op jit(solution)/shard_map/all_to_all | solution.py:85
  396.8 8.3 %all-to-all-start.1 = ((bf16[64,96,128]{2,1,0:T(8,128)(2,1)}), bf16[64,96,128]{2,1,0:T(8,128)(2,1)}, u32[]{:S(2)}, u32[]{:S(2)}) async-start(bf16[64,96,128]{2,1,0:T(8,128)(2,1)} %bitcast.177), calls=%async_computation.1 | async-start | bytes 3145728 | tf_op jit(solution)/shard_map/all_to_all | solution.py:86
  405.2 38.4 %all-to-all-done.1 = bf16[64,96,128]{2,1,0:T(8,128)(2,1)} async-done(((bf16[64,96,128]{2,1,0:T(8,128)(2,1)}), bf16[64,96,128]{2,1,0:T(8,128)(2,1)}, u32[]{:S(2)}, u32[]{:S(2)}) %all-to-all-start.1) | async-done | bytes 1572896 | tf_op jit(solution)/shard_map/all_to_all | solution.py:86
  445.1 7.4 %all-to-all-start.3 = ((bf16[64,96,128]{2,1,0:T(8,128)(2,1)}), bf16[64,96,128]{2,1,0:T(8,128)(2,1)S(1)}, u32[]{:S(2)}, u32[]{:S(2)}) async-start(bf16[64,96,128]{2,1,0:T(8,128)(2,1)} %bitcast.44), calls=%async_computation.3 | async-start | bytes 3145728 | tf_op jit(solution)/shard_map/all_to_all | solution.py:87
  454.1 36.7 %all-to-all-done.3 = bf16[64,96,128]{2,1,0:T(8,128)(2,1)S(1)} async-done(((bf16[64,96,128]{2,1,0:T(8,128)(2,1)}), bf16[64,96,128]{2,1,0:T(8,128)(2,1)S(1)}, u32[]{:S(2)}, u32[]{:S(2)}) %all-to-all-start.3) | async-done | bytes 1572896 | tf_op jit(solution)/shard_map/all_to_all | solution.py:87
  490.8 28.7 %while.51 = (s32[]{:T(128)}, f32[1,256]{1,0:T(1,128)S(1)}, f32[1,256]{1,0:T(1,128)S(1)}, f32[1,256,128]{2,1,0:T(8,128)S(1)}, s32[]{:T(128)}, /*index=5*/s32[256]...) while((s32[]{:T(128)}, f32[1,256]{1,0:T(1,128)S(1)}, ...), condition=%wide.region_11.12_spmd, body=%wide.region_6.11_spmd.sunk | while | flops 68748288 | bytes 2190645 | solution.py:141
  519.5 30.0 %while.52 = (s32[]{:T(128)}, f32[1,256]{1,0:T(1,128)S(1)}, f32[1,256]{1,0:T(1,128)S(1)}, f32[1,256,128]{2,1,0:T(8,128)S(1)}, s32[]{:T(128)}, /*index=5*/s32[256]...) while((s32[]{:T(128)}, f32[1,256]{1,0:T(1,128)S(1)}, ...), condition=%wide.region_18.19_spmd, body=%wide.region_13.18_spmd.sunk | while | flops 68748288 | bytes 2190645 | solution.py:141
  520.1 1.8 conditional.7
  537.6 1.8 conditional.7
  549.5 29.9 %while.53 = (s32[]{:T(128)}, f32[1,256]{1,0:T(1,128)S(1)}, f32[1,256]{1,0:T(1,128)S(1)}, f32[1,256,128]{2,1,0:T(8,128)S(1)}, s32[]{:T(128)}, /*index=5*/s32[256]...) while((s32[]{:T(128)}, f32[1,256]{1,0:T(1,128)S(1)}, ...), condition=%wide.region_25.26_spmd, body=%wide.region_20.25_spmd.sunk | while | flops 68748288 | bytes 2190645 | solution.py:141
  560.1 1.8 conditional.8
  562.6 1.8 conditional.8
  565.0 1.8 conditional.8
  572.5 1.8 conditional.8
  575.0 1.8 conditional.8
  (348 shorter events, 135.5 us)
Async XLA Ops:
  7.4 208.2 %all-reduce.2.cloned.1.call-start = ((), (), s32[]{:S(2)}) async-start(), calls=%async_computation.4 | async-start | bytes 6291456 | tf_op jit(solution)/shard_map/psum | solution.py:53
  125.7 175.6 %all-gather.4.cloned.1.call-start = ((), (), s32[]{:S(2)}) async-start(), calls=%async_computation.5 | async-start | bytes 6389760 | tf_op jit(solution)/shard_map/all_gather | solution.py:59
  223.4 53.9 %all-to-all-start = ((bf16[64,2,6144]{2,1,0:T(2,128)(2,1)}), bf16[64,2,6144]{2,1,0:T(2,128)(2,1)S(1)}, u32[]{:S(2)}, u32[]{:S(2)}) async-start(bf16[64,2,6144]{2,1,0:T(2,128)(2,1)} %reshape.275), calls=%async_computation | async-start | bytes 3145728 | tf_op jit(solution)/shard_map/all_to_all | solution.py:54
  236.2 96.5 %all-gather.6.cloned.1.call-start = ((), (), s32[]{:S(2)}) async-start(), calls=%async_computation.6 | async-start | bytes 2654208 | tf_op jit(solution)/shard_map/all_gather | solution.py:62
  297.3 1.4 copy-start.1
  335.0 1.7 copy-start
  336.6 0.7 copy-start.2
  342.5 13.8 %copy-start.3 = (f32[128]{0:T(128)S(1)}, f32[128]{0:T(128)}, u32[]{:S(2)}) copy-start(f32[128]{0:T(128)} %param.23) | copy-start | bytes 1540
  342.5 52.9 %all-to-all-start.2 = ((bf16[64,96,128]{2,1,0:T(8,128)(2,1)}), bf16[64,96,128]{2,1,0:T(8,128)(2,1)}, u32[]{:S(2)}, u32[]{:S(2)}) async-start(bf16[64,96,128]{2,1,0:T(8,128)(2,1)} %bitcast.178), calls=%async_computation.2 | async-start | bytes 3145728 | tf_op jit(solution)/shard_map/all_to_all | solution.py:85
  357.4 47.7 %slice-start = ((bf16[2,96,6144]{2,1,0:T(8,128)(2,1)}), bf16[2,96,1024]{2,1,0:T(8,128)(2,1)S(1)}, s32[]{:S(2)}) async-start(bf16[2,96,6144]{2,1,0:T(8,128)(2,1)} %all-gather.6.cloned.1.call-done), calls=%async_computation.7 | async-start | bytes 786432 | tf_op jit(solution)/shard_map/slice | solution.py:75
  396.8 46.9 %all-to-all-start.1 = ((bf16[64,96,128]{2,1,0:T(8,128)(2,1)}), bf16[64,96,128]{2,1,0:T(8,128)(2,1)}, u32[]{:S(2)}, u32[]{:S(2)}) async-start(bf16[64,96,128]{2,1,0:T(8,128)(2,1)} %bitcast.177), calls=%async_computation.1 | async-start | bytes 3145728 | tf_op jit(solution)/shard_map/all_to_all | solution.py:86
  445.1 45.7 %all-to-all-start.3 = ((bf16[64,96,128]{2,1,0:T(8,128)(2,1)}), bf16[64,96,128]{2,1,0:T(8,128)(2,1)S(1)}, u32[]{:S(2)}, u32[]{:S(2)}) async-start(bf16[64,96,128]{2,1,0:T(8,128)(2,1)} %bitcast.44), calls=%async_computation.3 | async-start | bytes 3145728 | tf_op jit(solution)/shard_map/all_to_all | solution.py:87
Sparse Core Ops, SparseCore 0:
  125.9 89.6 all-reduce.1
  306.4 26.2 all-gather.5
Sparse Core Ops, SparseCore 1:
  129.2 96.6 all-gather.3
where the time goes:
time: 590 us; the launch traced here: 588 us
  waiting for transfers between devices  270 us (46%)
  local copies, waits for them, and re-layouts  81.6 us (14%)
  matrix products  61.3 us (10%)
  other arithmetic  49.3 us (8%)
  blocking collectives  43.1 us (7%)
  starting transfers between devices  41.8 us (7%)
  loops' own time  25.6 us (4%)
  between operations  15.3 us (3%)
    psum x1, waiting for transfers between devices, shards(): summed = lax.psum(partial_rows.astype(jnp.bfloat16), 'tensor')  89.2 us
    all_gather x1, blocking collectives, shards(): all_ids = lax.all_gather(token_ids, 'context', axis=1, tiled=True)  43.1 us
    dot_general x35, matrix products, attend(): jnp.einsum('uqd,ukd->uqk', query_tile, key_tile, preferred_element_type=j...  41.2 us
    all_to_all x1, waiting for transfers between devices, shards(): lax.all_to_all(summed, 'context', split_axis=2, concat_axis=0, tiled=True)  40.8 us
    all_to_all x1, waiting for transfers between devices, shards(): lax.all_to_all(key_heads, 'context', split_axis=0, concat_axis=1, tiled=T...  38.4 us
    all_to_all x1, waiting for transfers between devices, shards(): lax.all_to_all(queries, 'context', split_axis=0, concat_axis=1, tiled=True)  38 us
    all_to_all x1, waiting for transfers between devices, shards(): lax.all_to_all(values, 'context', split_axis=0, concat_axis=1, tiled=True)  36.7 us
    gather x1, local copies, waits for them, and re-layouts, shards(): jnp.take(embed_table, jnp.clip(local_ids, 0, vocab_part - 1), axis=1)  35.7 us
  transfers between devices with their start and end apart: 7, of which 6 were waited for; matrix products, arithmetic and copies ran while one was open for 6% of the time, Pallas kernels for 0%

commit v1 on v0

v1 whole, which is shorter than its diff:
```python
import functools

import jax
import jax.numpy as jnp
from jax import lax
from jax.experimental import pallas as pl
from jax.experimental.pallas import tpu as pltpu
from jax.sharding import PartitionSpec as P

QH = 32
KVH = 8
HD = 128
ROPE_BASE = 1000000.0
EPSILON = 1e-06
NEGATIVE = -1e30
MESH = pl.DeviceIdType.MESH
VMEM_LIMIT = 60 * 1024 * 1024


def rope_tables(positions, width):
    half_width = width // 2
    exponent = jnp.arange(half_width, dtype=jnp.float32) * (2.0 / width)
    inverse = jnp.exp(-exponent * jnp.log(jnp.float32(ROPE_BASE)))
    angles = positions.astype(jnp.float32)[:, None] * inverse[None, :]
    angles = jnp.concatenate([angles, angles], axis=-1)
    return (jnp.cos(angles), jnp.sin(angles))


def remote(src, dst, send_sem, recv_sem, t, c):
    return pltpu.make_async_remote_copy(
        src_ref=src, dst_ref=dst, send_sem=send_sem, recv_sem=recv_sem,
        device_id=(t, c), device_id_type=MESH)


def greet(barrier, t, c, me_t, me_c):
    own = jnp.logical_and(t == me_t, c == me_c)

    @pl.when(jnp.logical_not(own))
    def _():
        pl.semaphore_signal(barrier, inc=1, device_id=(t, c), device_id_type=MESH)

    return own.astype(jnp.int32)


K0 = 8
V0 = 72
W_CHUNKS = 8


def attention_kernel(x_ref, w_hbm, cos_ref, sin_ref, qg_ref, kg_ref, o_ref,
                     w_buf, acc_ref, heads, blocks, w_sem,
                     s1_send, s1_recv, s2_send, s2_recv, s3_send, s3_recv,
                     s4_send, s4_recv):
    t = lax.axis_index("tensor")
    c = lax.axis_index("context")
    x, k = t // 2, t % 2
    chunk = w_buf.shape[1]
    w_copies = [
        pltpu.make_async_copy(w_hbm.at[pl.ds(i * chunk, chunk)], w_buf.at[i], w_sem.at[i])
        for i in range(W_CHUNKS)
    ]
    for w_copy in w_copies:
        w_copy.start()

    head_u = c % QH
    group_u = head_u // 4
    y4 = head_u % 4
    barrier = pltpu.get_barrier_semaphore()
    kept = jnp.int32(0)
    for i in range(8):
        kept += greet(barrier, head_u // 6, 8 * t + i, t, c)
    for i in range(2):
        kept += greet(barrier, (QH + group_u) // 6, 8 * t + 2 * y4 + i, t, c)
        kept += greet(barrier, (QH + KVH + group_u) // 6, 8 * t + 2 * y4 + i, t, c)
    for d in range(1, 4):
        pl.semaphore_signal(barrier, inc=1, device_id=(t, c - y4 + (y4 + d) % 4), device_id_type=MESH)
    for d in range(1, 8):
        pl.semaphore_signal(barrier, inc=1, device_id=((t + d) % 8, c), device_id_type=MESH)

    for i in range(W_CHUNKS):
        w_copies[i].wait()
        part = jnp.dot(x_ref[:, i * chunk:(i + 1) * chunk], w_buf[i],
                       preferred_element_type=jnp.float32)
        if i == 0:
            acc_ref[...] = part
        else:
            acc_ref[...] += part

    cos_t, sin_t = cos_ref[...], sin_ref[...]
    for j in range(6):
        head = 6 * t + j
        gain = jnp.where(head < QH, qg_ref[...], kg_ref[...])
        for s in range(2):
            raw = acc_ref[96 * s:96 * s + 96, 128 * j:128 * j + 128].astype(jnp.bfloat16)
            wide = raw.astype(jnp.float32)
            mean_sq = jnp.mean(wide * wide, axis=-1, keepdims=True)
            scaled = wide * lax.rsqrt(mean_sq + EPSILON) * gain
            turned = scaled * cos_t + pltpu.roll(scaled, 64, 1) * sin_t
            heads[6 * s + j] = jnp.where(head < QH + KVH, turned, wide).astype(jnp.bfloat16)

    pl.semaphore_wait(barrier, 22 - kept)

    def stage1(b, start):
        s, j = b // 6, b % 6
        head = 6 * t + j
        is_q = head < QH
        i = jnp.maximum(head - QH, 0)
        kind, group = i // KVH, i % KVH
        to_c = s * QH + jnp.where(is_q, head, 4 * group + (c % 8) // 2)
        to_t = c // 8
        slot = jnp.where(is_q, c % 8, K0 + 64 * kind + c)
        sem = jnp.where(is_q, c % 8, 8 + 2 * kind + c % 2)
        own = jnp.logical_and(to_t == t, to_c == c)
        far = remote(heads.at[b], blocks.at[slot], s1_send.at[b], s1_recv.at[sem], to_t, to_c)

        @pl.when(own)
        def _():
            if start:
                pltpu.make_async_copy(heads.at[b], blocks.at[slot], s1_recv.at[sem]).start()

        @pl.when(jnp.logical_not(own))
        def _():
            if start:
                far.start()
            else:
                far.wait_send()

    def land(dst, sem):
        pltpu.make_async_copy(dst, dst, sem).wait()

    for b in range(12):
        stage1(b, True)
    base = 8 * t + 2 * y4
    for i in range(2):
        land(blocks.at[K0 + base + i], s1_recv.at[8 + i])
        land(blocks.at[V0 + base + i], s1_recv.at[10 + i])

    def stage2(kind, d):
        first = (K0, V0)[kind] + base
        peer = (y4 + d) % 4
        return remote(blocks.at[pl.ds(first, 2)], blocks.at[pl.ds(first, 2)],
                      s2_send.at[kind, d], s2_recv.at[kind, y4], t, c - y4 + peer)

    for kind in range(2):
        for d in range(1, 4):
            stage2(kind, d).start()
    for kind in range(2):
        for d in range(1, 4):
            peer = (y4 + d) % 4
            land(blocks.at[pl.ds((K0, V0)[kind] + 8 * t + 2 * peer, 2)], s2_recv.at[kind, peer])

    def slab(kind, tt):
        return blocks.at[pl.ds((K0, V0)[kind] + 8 * tt, 8)]

    def along_x(kind, of, to, n):
        return remote(slab(kind, 2 * of + k), slab(kind, 2 * of + k),
                      s3_send.at[n], s3_recv.at[kind, of], 2 * to + k, c)

    def arrived_x(kind, of):
        land(slab(kind, 2 * of + k), s3_recv.at[kind, of])

    def across(kind, of):
        return remote(slab(kind, 2 * of + k), slab(kind, 2 * of + k),
                      s4_send.at[kind, of], s4_recv.at[kind, of], 2 * x + 1 - k, c)

    def across_here(kind, of):
        last = jnp.where(k == 0, x, x - 1)
        return of <= last

    def hand_on(kind, of):
        @pl.when(across_here(kind, of))
        def _():
            across(kind, of).start()

    own_list = {
        0: [(0, 0, 1), (1, 0, 1), (0, 0, 3), (1, 0, 3)],
        1: [(1, 1, 0), (0, 1, 2), (1, 1, 2)],
        2: [(0, 2, 3), (1, 2, 3)],
        3: [],
    }
    relay_list = {0: [(1, 1, 3)], 1: [(0, 0, 2)], 2: [(0, 1, 3)], 3: [(1, 0, 2)]}
    get_list = {
        0: [],
        1: [(0, 0), (1, 0)],
        2: [(0, 1), (1, 1), (0, 0), (1, 0)],
        3: [(1, 0), (0, 0), (0, 2), (1, 2), (0, 1), (1, 1)],
    }
    for xx in range(4):
        @pl.when(x == xx)
        def _(xx=xx):
            for n, (kind, of, to) in enumerate(own_list[xx]):
                along_x(kind, of, to, n).start()
            for kind in range(2):
                @pl.when(k == 0)
                def _():
                    across(kind, xx).start()
            done = set()
            for n, (kind, of, to) in enumerate(relay_list[xx]):
                arrived_x(kind, of)
                done.add((kind, of))
                along_x(kind, of, to, len(own_list[xx]) + n).start()
                if of < xx:
                    across(kind, of).start()
            for kind, of in get_list[xx]:
                if (kind, of) not in done:
                    arrived_x(kind, of)
                    across(kind, of).start()

    for of in range(4):
        for kind in range(2):
            @pl.when(jnp.where(k == 1, of <= x, of < x))
            def _():
                land(slab(kind, 2 * of + 1 - k), s4_recv.at[kind, of])

    for i in range(8):
        land(blocks.at[i], s1_recv.at[i])

    score_scale = HD ** (-0.5)
    rows = 256

    def update(state, q, keys, vals, mask):
        old_max, old_total, old_acc = state
        scores = lax.dot_general(q, keys, (((1,), (1,)), ((), ())),
                                 preferred_element_type=jnp.float32) * score_scale
        if mask is not None:
            scores = jnp.where(mask, scores, NEGATIVE)
        new_max = jnp.maximum(old_max, jnp.max(scores, axis=-1, keepdims=True))
        weights = jnp.exp(scores - new_max)
        shrink = jnp.exp(old_max - new_max)
        new_total = old_total * shrink + jnp.sum(weights, axis=-1, keepdims=True)
        new_acc = old_acc * shrink + jnp.dot(
            weights.astype(jnp.bfloat16), vals, preferred_element_type=jnp.float32)
        return new_max, new_total, new_acc

    for i in range(3):
        q = blocks[0:8].reshape(768, HD)[rows * i:rows * (i + 1)]
        width = rows * (i + 1)
        keys = blocks[pl.ds(K0 + 8 * t, 8)].reshape(768, HD)[:width]
        vals = blocks[pl.ds(V0 + 8 * t, 8)].reshape(768, HD)[:width]
        mask = (lax.broadcasted_iota(jnp.int32, (rows, width), 1)
                <= lax.broadcasted_iota(jnp.int32, (rows, width), 0) + rows * i)
        state = (jnp.full((rows, 1), NEGATIVE, jnp.float32),
                 jnp.zeros((rows, 1), jnp.float32),
                 jnp.zeros((rows, HD), jnp.float32))
        state = update(state, q, keys, vals, mask)

        def step(tt, state, q=q):
            keys = blocks[pl.ds(K0 + 8 * tt, 8)].reshape(768, HD)
            vals = blocks[pl.ds(V0 + 8 * tt, 8)].reshape(768, HD)
            return update(state, q, keys, vals, None)

        _, total, acc = lax.fori_loop(0, t, step, state)
        o_ref[0, rows * i:rows * (i + 1), :] = (acc / total).astype(jnp.bfloat16)

    for b in range(12):
        stage1(b, False)
    for kind in range(2):
        for d in range(1, 4):
            stage2(kind, d).wait_send()
    for xx in range(4):
        @pl.when(x == xx)
        def _(xx=xx):
            sends = own_list[xx] + relay_list[xx]
            for n, (kind, of, to) in enumerate(sends):
                along_x(kind, of, to, n).wait_send()
    for of in range(4):
        for kind in range(2):
            @pl.when(across_here(kind, of))
            def _():
                across(kind, of).wait_send()


def attention(normed, w_all, cos_t, sin_t, q_gain, k_gain):
    vmem = pl.BlockSpec(memory_space=pltpu.VMEM)
    dma = pltpu.SemaphoreType.DMA
    return pl.pallas_call(
        attention_kernel,
        out_shape=jax.ShapeDtypeStruct((1, 768, HD), jnp.bfloat16),
        in_specs=[vmem, pl.BlockSpec(memory_space=pl.ANY), vmem, vmem, vmem, vmem],
        out_specs=vmem,
        scratch_shapes=[
            pltpu.VMEM((W_CHUNKS, 4096 // W_CHUNKS, 768), jnp.bfloat16),
            pltpu.VMEM((192, 768), jnp.float32),
            pltpu.VMEM((12, 96, HD), jnp.bfloat16),
            pltpu.VMEM((136, 96, HD), jnp.bfloat16),
            dma((W_CHUNKS,)),
            dma((12,)), dma((12,)),
            dma((2, 4)), dma((2, 4)),
            dma((6,)), dma((2, 4)),
            dma((2, 4)), dma((2, 4)),
        ],
        compiler_params=pltpu.CompilerParams(
            collective_id=1, has_side_effects=True, vmem_limit_bytes=VMEM_LIMIT),
        name="project_exchange_attend",
    )(normed, w_all, cos_t, sin_t, q_gain, k_gain)


def feature_norm(embedded, input_gain):
    hidden = embedded.astype(jnp.float32)
    mean_sq = jnp.mean(hidden * hidden, axis=0, keepdims=True)
    return (hidden * lax.rsqrt(mean_sq + EPSILON) * input_gain[:, None, None]).astype(jnp.bfloat16)


def shards(token_ids, embed_table, input_gain, w_qkv, q_gain, k_gain):
    tensor_rank = lax.axis_index("tensor")
    context_rank = lax.axis_index("context")
    seq_count, local_len = token_ids.shape
    width_part, vocab_part = embed_table.shape
    w_all = lax.all_gather(w_qkv, "context", axis=0, tiled=True)
    all_ids = lax.all_gather(token_ids, "context", axis=1, tiled=True)
    local_ids = all_ids - tensor_rank * vocab_part
    inside = (local_ids >= 0) & (local_ids < vocab_part)
    picked = jnp.take(embed_table, jnp.clip(local_ids, 0, vocab_part - 1), axis=1)
    partial_rows = jnp.where(inside[None], picked.astype(jnp.float32), 0.0)
    summed = lax.psum(partial_rows.astype(jnp.bfloat16), "tensor")
    embedded = lax.all_to_all(summed, "context", split_axis=2, concat_axis=0, tiled=True)
    normed = feature_norm(embedded, input_gain)
    normed = jnp.transpose(normed, (1, 2, 0)).reshape(seq_count * local_len, -1)
    positions = context_rank * local_len + jnp.arange(local_len, dtype=jnp.int32)
    cos_t, sin_t = rope_tables(positions, HD)
    sin_t = jnp.concatenate([-sin_t[:, :64], sin_t[:, 64:]], axis=-1)
    return attention(normed, w_all, cos_t, sin_t, q_gain[None], k_gain[None])


def solution(mesh):
    return jax.shard_map(
        shards,
        mesh=mesh,
        in_specs=(P(None, "context"), P("context", "tensor"), P(), P("context", "tensor"), P(), P()),
        out_specs=P("context", "tensor", None),
        check_vma=False,
    )
```

time: 590 us -> 376 us (0.64)
  the two profiles are of different devices: /device:TPU:15 before, /device:TPU:63 now
where the time goes in v1:
time: 376 us; the launch traced here: 375 us
  waiting for transfers between devices  128 us (34%)
  local copies, waits for them, and re-layouts  78.3 us (21%)
  Pallas kernels  64.2 us (17%)
  blocking collectives  42.7 us (11%)
  other arithmetic  34.8 us (9%)
  between operations  15 us (4%)
  starting transfers between devices  12.7 us (3%)
    psum x1, waiting for transfers between devices, shards(): summed = lax.psum(partial_rows.astype(jnp.bfloat16), 'tensor')  89 us
    pallas_call x1, Pallas kernels, attention(): pl.pallas_call(attention_kernel, out_shape=jax.ShapeDtypeStruct((1, 768,...  64.2 us
    all_gather x1, blocking collectives, shards(): all_ids = lax.all_gather(token_ids, 'context', axis=1, tiled=True)  42.7 us
    all_to_all x1, waiting for transfers between devices, shards(): lax.all_to_all(summed, 'context', split_axis=2, concat_axis=0, tiled=True)  38.1 us
    gather x1, local copies, waits for them, and re-layouts, shards(): jnp.take(embed_table, jnp.clip(local_ids, 0, vocab_part - 1), axis=1)  35.7 us
    convert_element_type x1, other arithmetic, shards(): summed = lax.psum(partial_rows.astype(jnp.bfloat16), 'tensor')  29.7 us
    unnamed x8, local copies, waits for them, and re-layouts  19.7 us
    all_to_all x1, starting transfers between devices, shards(): lax.all_to_all(summed, 'context', split_axis=2, concat_axis=0, tiled=True)  12.7 us
  transfers between devices with their start and end apart: 3, of which 2 were waited for; matrix products, arithmetic and copies ran while one was open for 10% of the time, Pallas kernels for 0%

profile of v1, /device:TPU:63, one launch (start us, length us, event | category | flops | bytes accessed | tf_op | source)
XLA Modules:
  0.0 375.3 jit_solution(14693901258596045553)
XLA Ops:
  7.4 42.7 %all-gather = s32[64,96,2]{1,2,0:T(2,128)S(1)} all-gather(s32[1,96,2]{1,2,0:T(2,128)} %bitcast.45), channel_id=1, replica_groups=mesh['tensor'=8,'context'=64] {'context'}, dimensions={0}, use_global_device_ids=true | all-gather | bytes 49920 | tf_op jit(solution)/shard_map/all_gather | solution.py:310
  50.1 0.1 reshape.60
  50.2 0.1 compare_and_fusion
  50.4 5.8 %copy.50 = bf16[64,18992]{0,1:T(8,128)(2,1)} copy(bf16[64,18992]{1,0:T(8,128)(2,1)} %param.7) | data formatting | bytes 4861952 | tf_op args[1]
  56.2 1.8 copy.49
  58.0 0.1 reshape.61
  58.1 1.8 copy.48
  59.9 35.7 %gather_fusion = bf16[12288,64]{1,0:T(8,128)(2,1)S(1)} fusion(bf16[64,18992]{0,1:T(8,128)(2,1)} %copy.50, s32[12288]{0:T(1024)S(1)} %broadcast_clamp_fusion), kind=kCustom, calls=%fused_computation | custom fusion | bytes 3194880 | tf_op jit(solution)/shard_map/jit(_take)/gather | solution.py:313
  95.6 29.7 %fusion.2 = bf16[64,2,6144]{0,1,2:T(2,128)(2,1)} fusion(pred[2,6144]{0,1:T(8,128)(4,1)} %copy.49, pred[2,6144]{0,1:T(8,128)(4,1)} %copy.48, bf16[2,6144,64]{2,1,0:T(8,128)(2,1)S(1)} %bitcast.40), kind=kLoop, calls=%fused_computation.6 | loop fusion | flops 3145728 | bytes 3170304 | tf_op jit(solution)/shard_map/convert_element_type | solution.py:315
  125.3 0.0 all-reduce.2.cloned.1.call-update
  125.3 0.0 all-gather.3.cloned.1.call-start
  125.4 0.5 all-gather.3.cloned.1.call-update
  125.9 89.0 %all-reduce.2.cloned.1.call-done = bf16[64,2,6144]{0,1,2:T(2,128)(2,1)} async-done(((bf16[64,2,6144]{0,1,2:T(2,128)(2,1)}), bf16[64,2,6144]{0,1,2:T(2,128)(2,1)}) %all-reduce.2.cloned.1.call-update) | async-done | bytes 1572880 | tf_op jit(solution)/shard_map/psum | solution.py:315
  214.9 7.8 %reshape.62 = bf16[64,2,6144]{2,1,0:T(2,128)(2,1)} reshape(bf16[6144,2,64]{2,1,0:T(2,128)(2,1)} %bitcast.42) | data formatting | bytes 3145728
  222.7 12.7 %all-to-all-start = ((bf16[64,2,6144]{2,1,0:T(2,128)(2,1)}), bf16[64,2,6144]{2,1,0:T(2,128)(2,1)S(1)}, u32[]{:S(2)}, u32[]{:S(2)}) async-start(bf16[64,2,6144]{2,1,0:T(2,128)(2,1)} %reshape.62), calls=%async_computation | async-start | bytes 3145728 | tf_op jit(solution)/shard_map/all_to_all | solution.py:316
  235.4 0.1 broadcast_multiply_fusion
  235.5 0.9 fusion.4
  236.4 0.1 slice_negate_fusion
  236.4 0.7 pad_maximum_fusion.1.sin_ref
  237.1 38.1 %all-to-all-done = bf16[64,2,6144]{2,1,0:T(2,128)(2,1)S(1)} async-done(((bf16[64,2,6144]{2,1,0:T(2,128)(2,1)}), bf16[64,2,6144]{2,1,0:T(2,128)(2,1)S(1)}, u32[]{:S(2)}, u32[]{:S(2)}) %all-to-all-start) | async-done | bytes 1572896 | tf_op jit(solution)/shard_map/all_to_all | solution.py:316
  275.3 3.4 reshape.63
  278.7 6.3 %copy.52 = bf16[64,2,6144]{2,0,1:T(8,128)(2,1)S(1)} copy(bf16[64,2,6144]{0,1,2:T(2,128)(2,1)} %bitcast.38) | data formatting | bytes 3145728 | tf_op jit(solution)/shard_map/all_to_all | solution.py:316
  285.0 3.2 reshape.39
  288.2 6.7 %copy.53 = f32[64,64,2,96]{3,1,0,2:T(8,128)} copy(f32[64,64,2,96]{3,0,1,2:T(8,128)} %bitcast.36) | data formatting | bytes 6291456 | tf_op jit(solution)/shard_map/convert_element_type | solution.py:299
  294.9 0.4 multiply_reduce_fusion
  295.3 1.1 copy.57
  296.4 0.2 reduce_sum.18
  296.6 0.1 copy.55
  296.7 2.6 fusion.1
  299.3 2.7 copy.56
  302.0 64.2 %project_exchange_attend.1 = bf16[1,768,128]{2,1,0:T(8,128)(2,1)} custom-call(bf16[192,4096]{1,0:T(8,128)(2,1)} %bitcast.41, bf16[4096,768]{1,0:T(8,128)(2,1)} %all-gather.3.cloned.1.call-done.w_hbm, f32[96,128]{1,0:T(8,128)} %get-tuple-element.8.cos_ref, f32[96,128]{1,0:T(8,128)} %pad_maximum_fusion.1.sin_ref, f32[1,128]{1,0:T(1,128)} %bitcast.46, ...), custom_call_target="tpu_custom_call" | custom-call | tf_op jit(solution)/shard_map/project_exchange_attend/pallas_call | solution.py:276
  366.2 1.6 copy.67
  (12 shorter events, 0.1 us)
Async XLA Ops:
  7.4 207.5 %all-reduce.2.cloned.1.call-start = ((), (), s32[]{:S(2)}) async-start(), calls=%async_computation.1 | async-start | bytes 6291456 | tf_op jit(solution)/shard_map/psum | solution.py:315
  125.3 176.7 %all-gather.3.cloned.1.call-start = ((), (), s32[]{:S(2)}) async-start(), calls=%async_computation.2 | async-start | bytes 6389760 | tf_op jit(solution)/shard_map/all_gather | solution.py:309
  222.7 52.6 %all-to-all-start = ((bf16[64,2,6144]{2,1,0:T(2,128)(2,1)}), bf16[64,2,6144]{2,1,0:T(2,128)(2,1)S(1)}, u32[]{:S(2)}, u32[]{:S(2)}) async-start(bf16[64,2,6144]{2,1,0:T(2,128)(2,1)} %reshape.62), calls=%async_computation | async-start | bytes 3145728 | tf_op jit(solution)/shard_map/all_to_all | solution.py:316
  295.3 1.4 copy-start
Sparse Core Ops, SparseCore 0:
  125.4 89.3 all-reduce.1
Sparse Core Ops, SparseCore 1:
  128.8 97.1 all-gather.2

commit v2 on v1

--- a/solution.py
+++ b/solution.py
@@ -79,8 +79,9 @@
 
     for i in range(W_CHUNKS):
         w_copies[i].wait()
-        part = jnp.dot(x_ref[:, i * chunk:(i + 1) * chunk], w_buf[i],
-                       preferred_element_type=jnp.float32)
+        at = i % 4 * chunk
+        lhs = x_ref[:, i // 4, :, at:at + chunk].reshape(192, chunk)
+        part = jnp.dot(lhs, w_buf[i], preferred_element_type=jnp.float32)
         if i == 0:
             acc_ref[...] = part
         else:
@@ -295,27 +296,235 @@
     )(normed, w_all, cos_t, sin_t, q_gain, k_gain)
 
 
-def feature_norm(embedded, input_gain):
-    hidden = embedded.astype(jnp.float32)
-    mean_sq = jnp.mean(hidden * hidden, axis=0, keepdims=True)
-    return (hidden * lax.rsqrt(mean_sq + EPSILON) * input_gain[:, None, None]).astype(jnp.bfloat16)
+VOCAB_PART = 18992
+ZERO_ROW = VOCAB_PART
+
+
+def embed_kernel(ids_ref, table_ref, gain_ref, out_ref,
+                 rows_ref, ids_v, ids_t, ids_s, low, high,
+                 for_other, own, from_other, from_x, summed, pieces, wide_ref, normed,
+                 ids_send, ids_recv, idx_sem, rs4_send, rs4_recv, rsx_send, rsx_recv,
+                 a2a_send, a2a_recv, agx_send, agx_recv, agr_send, agr_recv, agp_send, agp_recv):
+    t = lax.axis_index("tensor")
+    c = lax.axis_index("context")
+    x, k = t // 2, t % 2
+    other = 2 * x + 1 - k
+    barrier = pltpu.get_barrier_semaphore()
+
+    @pl.loop(1, 64)
+    def _(i):
+        pl.semaphore_signal(barrier, inc=1, device_id=(t, (c + i) % 64), device_id_type=MESH)
+
+    for d in range(1, 8):
+        pl.semaphore_signal(barrier, inc=1, device_id=((t + d) % 8, c), device_id_type=MESH)
+
+    def transpose(block):
+        wide = block.astype(jnp.float32)
+        return jnp.concatenate([wide, wide], axis=0).T
+
+    full = VOCAB_PART // 128
+
+    def turn(first, last):
+        @pl.loop(first, last, unroll=2)
+        def _(b):
+            at = pl.multiple_of(b * 128, 128)
+            rows_ref[pl.ds(at, 128), :] = transpose(table_ref[:, pl.ds(at, 128)])
+
+    turn(0, full // 2)
+    pl.semaphore_wait(barrier, 70)
+
+    def send_ids(i):
+        return remote(ids_ref, ids_v.at[c], ids_send.at[i], ids_recv.at[c], t, (c + i) % 64)
+
+    @pl.loop(1, 64)
+    def _(i):
+        send_ids(i).start()
+
+    ids_v[c] = ids_ref[...]
+    turn(full // 2, full)
+    rest = VOCAB_PART - full * 128
+    tail = jnp.concatenate(
+        [table_ref[:, full * 128:].astype(jnp.float32), jnp.zeros((64, 128 - rest), jnp.float32)], axis=1)
+    rows_ref[full * 128:, :] = transpose(tail)
+
+    def land(dst, sem):
+        pltpu.make_async_copy(dst, dst, sem).wait()
+
+    @pl.loop(1, 64)
+    def _(i):
+        src = (c + i) % 64
+        land(ids_v.at[src], ids_recv.at[src])
+
+    local = ids_v[...] - t * VOCAB_PART
+    ids_t[...] = jnp.where(jnp.logical_and(local >= 0, local < VOCAB_PART), local, ZERO_ROW)
+    to_smem = pltpu.make_async_copy(ids_t, ids_s, idx_sem)
+    to_smem.start()
+    to_smem.wait()
+
+    first_half = lax.broadcasted_iota(jnp.int32, (16, 128), 1) < 64
+
+    def look_up(tp, dst, n):
+        s = tp // 4
+        start = 24 * (tp % 4)
+
+        @pl.loop(0, 32)
+        def _(half):
+            for m in range(2):
+                cc = 2 * half + m
+                for i in range(12):
+                    low[m, i:i + 1, :] = rows_ref[pl.ds(ids_s[cc, s, start + i], 1), :]
+                for i in range(12):
+                    high[m, i:i + 1, :] = rows_ref[pl.ds(ids_s[cc, s, start + 12 + i], 1), :]
+            for m in range(2):
+                dst[n, 2 * half + m] = jnp.where(first_half, low[m], high[m]).astype(jnp.bfloat16)
+
+    low[...] = jnp.zeros_like(low)
+    high[...] = jnp.zeros_like(high)
+
+    def to_other(n):
+        return remote(for_other.at[n], from_other.at[n], rs4_send.at[n], rs4_recv.at[n], other, c)
+
+    def to_chip(n, xx):
+        return remote(own.at[n], from_x.at[n], rsx_send.at[n], rsx_recv.at[n], 2 * xx + k, c)
+
+    for n, d in enumerate((2, 1, 3, 0)):
+        xx = (x + d) % 4
+        look_up(2 * xx + 1 - k, for_other, n)
+        to_other(n).start()
+        look_up(2 * xx + k, own, n)
+        land(from_other.at[n], rs4_recv.at[n])
+        own[n] = own[n] + from_other[n]
+        if d:
+            to_chip(n, xx).start()
+
+    for n in range(3):
+        land(from_x.at[n], rsx_recv.at[n])
+    summed[...] = (own[3] + from_x[0]) + (from_x[1] + from_x[2])
+
+    def send_rows(i):
+        peer = (c + i) % 64
+        return remote(summed.at[peer], pieces.at[c], a2a_send.at[i], a2a_recv.at[c], t, peer)
+
+    @pl.loop(1, 64)
+    def _(i):
+        send_rows(i).start()
+
+    pieces[c] = summed[c]
+
+    @pl.loop(1, 64)
+    def _(i):
+        src = (c + i) % 64
+        land(pieces.at[src], a2a_recv.at[src])
+
+    def add_squares(i, acc):
+        piece = pieces[i].astype(jnp.float32)
+        return acc + piece * piece
+
+    squares = lax.fori_loop(0, 64, add_squares, jnp.zeros((16, 128), jnp.float32))
+    sum_low = jnp.sum(jnp.where(first_half, squares, 0.0), axis=-1, keepdims=True)
+    sum_high = jnp.sum(jnp.where(first_half, 0.0, squares), axis=-1, keepdims=True)
+    scale_low = lax.rsqrt(sum_low / 4096 + EPSILON)
+    scale_high = lax.rsqrt(sum_high / 4096 + EPSILON)
+    for p in range(32):
+        even = pieces[2 * p].astype(jnp.float32)
+        odd = pieces[2 * p + 1].astype(jnp.float32)
+        gain = gain_ref[:, 128 * p:128 * p + 128]
+        low_rows = jnp.where(first_half, even, pltpu.roll(odd, 64, 1)) * scale_low * gain
+        high_rows = jnp.where(first_half, pltpu.roll(even, 64, 1), odd) * scale_high * gain
+        wide_ref[0:12, 128 * p:128 * p + 128] = low_rows[:12]
+        wide_ref[12:24, 128 * p:128 * p + 128] = high_rows[:12]
+    for h in range(2):
+        part = wide_ref[:, 2048 * h:2048 * h + 2048].astype(jnp.bfloat16)
+        normed[h] = part
+        out_ref[t, h] = part
+
+    right, left = 2 * ((x + 1) % 4) + k, 2 * ((x + 3) % 4) + k
+    across = 2 * ((x + 2) % 4) + k
+    to_right = remote(normed, out_ref.at[t], agx_send.at[0], agx_recv.at[0], right, c)
+    to_left = remote(normed, out_ref.at[t], agx_send.at[1], agx_recv.at[1], left, c)
+    to_right.start()
+    to_left.start()
+
+    def hand_over(src, tt, n):
+        return remote(src, out_ref.at[tt], agp_send.at[n], agp_recv.at[n], other, c)
+
+    hand_own = hand_over(normed, t, 0)
+    hand_own.start()
+    land(out_ref.at[left], agx_recv.at[0])
+    on_right = remote(out_ref.at[left, 0], out_ref.at[left, 0], agr_send.at[0], agr_recv.at[0], right, c)
+    on_right.start()
+    hand_left = hand_over(out_ref.at[left], left, 1)
+    hand_left.start()
+    land(out_ref.at[right], agx_recv.at[1])
+    on_left = remote(out_ref.at[right, 1], out_ref.at[right, 1], agr_send.at[1], agr_recv.at[1], left, c)
+    on_left.start()
+    hand_right = hand_over(out_ref.at[right], right, 2)
+    hand_right.start()
+    land(out_ref.at[across, 0], agr_recv.at[0])
+    land(out_ref.at[across, 1], agr_recv.at[1])
+    hand_across = hand_over(out_ref.at[across], across, 3)
+    hand_across.start()
+
+    flip = 1 - 2 * k
+    land(out_ref.at[t + flip], agp_recv.at[0])
+    land(out_ref.at[left + flip], agp_recv.at[1])
+    land(out_ref.at[right + flip], agp_recv.at[2])
+    land(out_ref.at[across + flip], agp_recv.at[3])
+
+    @pl.loop(1, 64)
+    def _(i):
+        send_ids(i).wait_send()
+        send_rows(i).wait_send()
+
+    for n, d in enumerate((2, 1, 3, 0)):
+        to_other(n).wait_send()
+        if d:
+            to_chip(n, (x + d) % 4).wait_send()
+    for copy in (to_right, to_left, on_right, on_left, hand_own, hand_left, hand_right, hand_across):
+        copy.wait_send()
+
+
+def embed(ids, table, gain):
+    vmem = pl.BlockSpec(memory_space=pltpu.VMEM)
+    dma = pltpu.SemaphoreType.DMA
+    slabs = (64, 16, 128)
+    return pl.pallas_call(
+        embed_kernel,
+        out_shape=jax.ShapeDtypeStruct((8, 2, 24, 2048), jnp.bfloat16),
+        in_specs=[vmem, vmem, vmem],
+        out_specs=vmem,
+        scratch_shapes=[
+            pltpu.VMEM((VOCAB_PART // 128 * 128 + 128, 128), jnp.float32),
+            pltpu.VMEM((64, 2, 128), jnp.int32),
+            pltpu.VMEM((64, 2, 128), jnp.int32),
+            pltpu.SMEM((64, 2, 128), jnp.int32),
+            pltpu.VMEM((2, 16, 128), jnp.float32),
+            pltpu.VMEM((2, 16, 128), jnp.float32),
+            pltpu.VMEM((4,) + slabs, jnp.bfloat16),
+            pltpu.VMEM((4,) + slabs, jnp.bfloat16),
+            pltpu.VMEM((4,) + slabs, jnp.bfloat16),
+            pltpu.VMEM((3,) + slabs, jnp.bfloat16),
+            pltpu.VMEM(slabs, jnp.bfloat16),
+            pltpu.VMEM(slabs, jnp.bfloat16),
+            pltpu.VMEM((24, 4096), jnp.float32),
+            pltpu.VMEM((2, 24, 2048), jnp.bfloat16),
+            dma((64,)), dma((64,)), dma,
+            dma((4,)), dma((4,)), dma((3,)), dma((3,)),
+            dma((64,)), dma((64,)),
+            dma((2,)), dma((2,)), dma((2,)), dma((2,)), dma((4,)), dma((4,)),
+        ],
+        compiler_params=pltpu.CompilerParams(
+            collective_id=0, has_side_effects=True, vmem_limit_bytes=VMEM_LIMIT),
+        name="look_up_scatter_norm",
+    )(ids, table, gain)
 
 
 def shards(token_ids, embed_table, input_gain, w_qkv, q_gain, k_gain):
-    tensor_rank = lax.axis_index("tensor")
     context_rank = lax.axis_index("context")
-    seq_count, local_len = token_ids.shape
-    width_part, vocab_part = embed_table.shape
+    local_len = token_ids.shape[1]
     w_all = lax.all_gather(w_qkv, "context", axis=0, tiled=True)
-    all_ids = lax.all_gather(token_ids, "context", axis=1, tiled=True)
-    local_ids = all_ids - tensor_rank * vocab_part
-    inside = (local_ids >= 0) & (local_ids < vocab_part)
-    picked = jnp.take(embed_table, jnp.clip(local_ids, 0, vocab_part - 1), axis=1)
-    partial_rows = jnp.where(inside[None], picked.astype(jnp.float32), 0.0)
-    summed = lax.psum(partial_rows.astype(jnp.bfloat16), "tensor")
-    embedded = lax.all_to_all(summed, "context", split_axis=2, concat_axis=0, tiled=True)
-    normed = feature_norm(embedded, input_gain)
-    normed = jnp.transpose(normed, (1, 2, 0)).reshape(seq_count * local_len, -1)
+    ids = jnp.pad(token_ids, ((0, 0), (0, 128 - local_len)))
+    normed = embed(ids, embed_table, input_gain[None])
     positions = context_rank * local_len + jnp.arange(local_len, dtype=jnp.int32)
     cos_t, sin_t = rope_tables(positions, HD)
     sin_t = jnp.concatenate([-sin_t[:, :64], sin_t[:, 64:]], axis=-1)

time: 376 us -> 177 us (0.47)
  waiting for transfers between devices: 128 us -> 13.7 us
  Pallas kernels: 64.2 us -> 145 us
  local copies, waits for them, and re-layouts: 78.3 us -> 2.86 us
  blocking collectives: 42.7 us -> 0 us
  other arithmetic: 34.8 us -> 1.76 us
  starting transfers between devices: 12.7 us -> 0.01 us
    psum x1 -> x0, waiting for transfers between devices: 89 us -> none  [shards(): summed = lax.psum(partial_rows.astype(jnp.bfloat16), 'tensor')]
    pallas_call x0 -> x1, Pallas kernels: none -> 79.6 us  [embed(): pl.pallas_call(embed_kernel, out_shape=jax.ShapeDtypeStruct((8, 2, 24, 20...]
    all_gather x1 -> x0, blocking collectives: 42.7 us -> none  [shards(): all_ids = lax.all_gather(token_ids, 'context', axis=1, tiled=True)]
    all_to_all x1 -> x0, waiting for transfers between devices: 38.1 us -> none  [shards(): lax.all_to_all(summed, 'context', split_axis=2, concat_axis=0, tiled=True)]
    gather x1 -> x0, local copies, waits for them, and re-layouts: 35.7 us -> none  [shards(): jnp.take(embed_table, jnp.clip(local_ids, 0, vocab_part - 1), axis=1)]
    convert_element_type x2 -> x0, other arithmetic: 32.3 us -> none  [the longest x1 29.7 us: shards(): summed = lax.psum(partial_rows.astype(jnp.bfloat16), 'tensor')]
    unnamed x8 -> x1, local copies, waits for them, and re-layouts: 19.7 us -> 1.62 us
    all_gather x1, waiting for transfers between devices: 0.01 us -> 13 us  [shards(): w_all = lax.all_gather(w_qkv, 'context', axis=0, tiled=True)]
  transfers between devices with their start and end apart: 3 -> 1, of which waited for: 2 -> 1; matrix products, arithmetic and copies ran while one was open for 10% -> 2% of each run, Pallas kernels for 0% -> 45%
where the time goes in v2:
time: 177 us
  Pallas kernels  145 us (82%)
  waiting for transfers between devices  13.7 us (8%)
  between operations  13.4 us (8%)
  local copies, waits for them, and re-layouts  2.86 us (2%)
    pallas_call x1, Pallas kernels, embed(): pl.pallas_call(embed_kernel, out_shape=jax.ShapeDtypeStruct((8, 2, 24, 20...  79.6 us
    pallas_call x1, Pallas kernels, attention(): pl.pallas_call(attention_kernel, out_shape=jax.ShapeDtypeStruct((1, 768,...  65.8 us
    all_gather x1, waiting for transfers between devices, shards(): w_all = lax.all_gather(w_qkv, 'context', axis=0, tiled=True)  13 us
  transfers between devices with their start and end apart: 1, of which 1 were waited for; matrix products, arithmetic and copies ran while one was open for 2% of the time, Pallas kernels for 45%

profile of v2, /device:TPU:63, one launch (start us, length us, event | category | flops | bytes accessed | tf_op | source)
XLA Modules:
  0.0 177.2 jit_solution(3988037340362860654)
XLA Ops:
  6.5 0.0 all-gather.2.cloned.1.call-start
  6.5 0.7 all-gather.2.cloned.1.call-update
  7.3 1.2 pad.4.ids_ref
  8.5 79.6 %look_up_scatter_norm.1.x_ref = bf16[8,2,24,2048]{3,2,1,0:T(8,128)(2,1)} custom-call(s32[2,128]{1,0:T(2,128)} %pad.4.ids_ref, bf16[64,18992]{1,0:T(8,128)(2,1)} %table_ref.1, f32[1,4096]{1,0:T(1,128)} %bitcast.3), custom_call_target="tpu_custom_call" | custom-call | tf_op jit(solution)/shard_map/look_up_scatter_norm/pallas_call | solution.py:491
  88.2 0.1 broadcast_multiply_fusion
  88.2 0.9 fusion
  89.1 0.1 slice_negate_fusion
  89.2 0.7 pad_maximum_fusion.1.sin_ref
  89.9 13.0 %all-gather.2.cloned.1.call-done.w_hbm = bf16[4096,768]{1,0:T(8,128)(2,1)} async-done(((bf16[64,768]{1,0:T(8,128)(2,1)}), bf16[4096,768]{1,0:T(8,128)(2,1)}) %all-gather.2.cloned.1.call-update) | async-done | bytes 6291472 | tf_op jit(solution)/shard_map/all_gather | solution.py:525
  102.9 65.8 %project_exchange_attend.1 = bf16[1,768,128]{2,1,0:T(8,128)(2,1)} custom-call(bf16[8,2,24,2048]{3,2,1,0:T(8,128)(2,1)} %look_up_scatter_norm.1.x_ref, bf16[4096,768]{1,0:T(8,128)(2,1)} %all-gather.2.cloned.1.call-done.w_hbm, f32[96,128]{1,0:T(8,128)} %get-tuple-element.8.cos_ref, f32[96,128]{1,0:T(8,128)} %pad_maximum_fusion.1.sin_ref, f32[1,128]{1,0:T(1,128)} %bitcast.4, ...), custom_call_target="tpu_custom_call" | custom-call | tf_op jit(solution)/shard_map/project_exchange_attend/pallas_call | solution.py:277
  168.7 1.6 copy.8
  (2 shorter events, 0.0 us)
Async XLA Ops:
  6.5 96.4 %all-gather.2.cloned.1.call-start = ((), (), s32[]{:S(2)}) async-start(), calls=%async_computation | async-start | bytes 6389760 | tf_op jit(solution)/shard_map/all_gather | solution.py:525
Sparse Core Ops, SparseCore 0:
  10.3 92.5 all-gather.1

commit v3 on v2

--- a/solution.py
+++ b/solution.py
@@ -50,7 +50,7 @@
 def attention_kernel(x_ref, w_hbm, cos_ref, sin_ref, qg_ref, kg_ref, o_ref,
                      w_buf, acc_ref, heads, blocks, w_sem,
                      s1_send, s1_recv, s2_send, s2_recv, s3_send, s3_recv,
-                     s4_send, s4_recv):
+                     s4_send, s4_recv, max_ref, total_ref, sum_ref):
     t = lax.axis_index("tensor")
     c = lax.axis_index("context")
     x, k = t // 2, t % 2
@@ -195,26 +195,6 @@
                 @pl.when(k == 0)
                 def _():
                     across(kind, xx).start()
-            done = set()
-            for n, (kind, of, to) in enumerate(relay_list[xx]):
-                arrived_x(kind, of)
-                done.add((kind, of))
-                along_x(kind, of, to, len(own_list[xx]) + n).start()
-                if of < xx:
-                    across(kind, of).start()
-            for kind, of in get_list[xx]:
-                if (kind, of) not in done:
-                    arrived_x(kind, of)
-                    across(kind, of).start()
-
-    for of in range(4):
-        for kind in range(2):
-            @pl.when(jnp.where(k == 1, of <= x, of < x))
-            def _():
-                land(slab(kind, 2 * of + 1 - k), s4_recv.at[kind, of])
-
-    for i in range(8):
-        land(blocks.at[i], s1_recv.at[i])
 
     score_scale = HD ** (-0.5)
     rows = 256
@@ -233,6 +213,8 @@
             weights.astype(jnp.bfloat16), vals, preferred_element_type=jnp.float32)
         return new_max, new_total, new_acc
 
+    for i in range(8):
+        land(blocks.at[i], s1_recv.at[i])
     for i in range(3):
         q = blocks[0:8].reshape(768, HD)[rows * i:rows * (i + 1)]
         width = rows * (i + 1)
@@ -243,14 +225,44 @@
         state = (jnp.full((rows, 1), NEGATIVE, jnp.float32),
                  jnp.zeros((rows, 1), jnp.float32),
                  jnp.zeros((rows, HD), jnp.float32))
-        state = update(state, q, keys, vals, mask)
-
-        def step(tt, state, q=q):
-            keys = blocks[pl.ds(K0 + 8 * tt, 8)].reshape(768, HD)
-            vals = blocks[pl.ds(V0 + 8 * tt, 8)].reshape(768, HD)
+        max_ref[i], total_ref[i], sum_ref[i] = update(state, q, keys, vals, mask)
+
+    def attend(i, first, count):
+        q = blocks[0:8].reshape(768, HD)[rows * i:rows * (i + 1)]
+
+        def step(of, state):
+            keys = blocks[pl.ds(K0 + 8 * (2 * of + first), 8)].reshape(768, HD)
+            vals = blocks[pl.ds(V0 + 8 * (2 * of + first), 8)].reshape(768, HD)
             return update(state, q, keys, vals, None)
 
-        _, total, acc = lax.fori_loop(0, t, step, state)
+        return lax.fori_loop(0, count, step, (max_ref[i], total_ref[i], sum_ref[i]))
+
+    for xx in range(4):
+        @pl.when(x == xx)
+        def _(xx=xx):
+            done = set()
+            for n, (kind, of, to) in enumerate(relay_list[xx]):
+                arrived_x(kind, of)
+                done.add((kind, of))
+                along_x(kind, of, to, len(own_list[xx]) + n).start()
+                if of < xx:
+                    across(kind, of).start()
+            for kind, of in get_list[xx]:
+                if (kind, of) not in done:
+                    arrived_x(kind, of)
+                    across(kind, of).start()
+
+    for i in range(3):
+        max_ref[i], total_ref[i], sum_ref[i] = attend(i, k, x)
+
+    for of in range(4):
+        for kind in range(2):
+            @pl.when(jnp.where(k == 1, of <= x, of < x))
+            def _():
+                land(slab(kind, 2 * of + 1 - k), s4_recv.at[kind, of])
+
+    for i in range(3):
+        _, total, acc = attend(i, 1 - k, x + k)
         o_ref[0, rows * i:rows * (i + 1), :] = (acc / total).astype(jnp.bfloat16)
 
     for b in range(12):
@@ -289,6 +301,9 @@
             dma((2, 4)), dma((2, 4)),
             dma((6,)), dma((2, 4)),
             dma((2, 4)), dma((2, 4)),
+            pltpu.VMEM((3, 256, 1), jnp.float32),
+            pltpu.VMEM((3, 256, 1), jnp.float32),
+            pltpu.VMEM((3, 256, HD), jnp.float32),
         ],
         compiler_params=pltpu.CompilerParams(
             collective_id=1, has_side_effects=True, vmem_limit_bytes=VMEM_LIMIT),
@@ -300,13 +315,17 @@
 ZERO_ROW = VOCAB_PART
 
 
-def embed_kernel(ids_ref, table_ref, gain_ref, out_ref,
-                 rows_ref, ids_v, ids_t, ids_s, low, high,
+def embed_kernel(ids_ref, table_ref, gain_ref, w_ref, out_ref, w_out,
+                 rows_ref, ids_v, ids_t, ids_s, pairs,
                  for_other, own, from_other, from_x, summed, pieces, wide_ref, normed,
                  ids_send, ids_recv, idx_sem, rs4_send, rs4_recv, rsx_send, rsx_recv,
-                 a2a_send, a2a_recv, agx_send, agx_recv, agr_send, agr_recv, agp_send, agp_recv):
+                 a2a_send, a2a_recv, agx_send, agx_recv, agr_send, agr_recv, agp_send, agp_recv,
+                 w_send, w_recv, w_sem):
     t = lax.axis_index("tensor")
     c = lax.axis_index("context")
+    z, y = c // 8, c % 8
+    keep_w = pltpu.make_async_copy(w_ref, w_out.at[z, y], w_sem)
+    keep_w.start()
     x, k = t // 2, t % 2
     other = 2 * x + 1 - k
     barrier = pltpu.get_barrier_semaphore()
@@ -333,6 +352,9 @@
     turn(0, full // 2)
     pl.semaphore_wait(barrier, 70)
 
+    def land(dst, sem):
+        pltpu.make_async_copy(dst, dst, sem).wait()
+
     def send_ids(i):
         return remote(ids_ref, ids_v.at[c], ids_send.at[i], ids_recv.at[c], t, (c + i) % 64)
 
@@ -340,6 +362,41 @@
     def _(i):
         send_ids(i).start()
 
+    def w_block(stage, half, at):
+        if (stage == 0) == (half == 0):
+            return w_out.at[z, at, 0] if half == 0 else w_out.at[pl.ds(0, 8), at, 1]
+        return w_out.at[at, pl.ds(0, 8), 0] if half == 0 else w_out.at[at, y, 1]
+
+    def w_step(stage, half, up, step):
+        here = y if (stage == 0) == (half == 0) else z
+        sign = 1 if up else -1
+        block = w_block(stage, half, (here - sign * step) % 8)
+        to = (here + sign) % 8
+        peer = 8 * z + to if (stage == 0) == (half == 0) else 8 * to + y
+        n = step if up else 4 + step
+
+        def copy():
+            return remote(w_ref.at[half] if (stage, step) == (0, 0) else block, block,
+                          w_send.at[stage, half, n], w_recv.at[stage, half, n], t, peer)
+
+        return copy, w_block(stage, half, (here - sign * (step + 1)) % 8), w_recv.at[stage, half, n]
+
+    w_rings = [(half, up) for half in range(2) for up in (True, False)]
+
+    def pump(n):
+        for step, starting in ((n - 1, False), (n, True)):
+            stage, at = step // 4, step % 4
+            if not 0 <= stage < 2:
+                continue
+            for half, up in w_rings:
+                if at < (4 if up else 3):
+                    copy, arriving, sem = w_step(stage, half, up, at)
+                    if starting:
+                        copy().start()
+                    else:
+                        land(arriving, sem)
+
+    pump(0)
     ids_v[c] = ids_ref[...]
     turn(full // 2, full)
     rest = VOCAB_PART - full * 128
@@ -347,39 +404,46 @@
         [table_ref[:, full * 128:].astype(jnp.float32), jnp.zeros((64, 128 - rest), jnp.float32)], axis=1)
     rows_ref[full * 128:, :] = transpose(tail)
 
-    def land(dst, sem):
-        pltpu.make_async_copy(dst, dst, sem).wait()
+    pump(1)
 
     @pl.loop(1, 64)
     def _(i):
         src = (c + i) % 64
         land(ids_v.at[src], ids_recv.at[src])
 
-    local = ids_v[...] - t * VOCAB_PART
-    ids_t[...] = jnp.where(jnp.logical_and(local >= 0, local < VOCAB_PART), local, ZERO_ROW)
-    to_smem = pltpu.make_async_copy(ids_t, ids_s, idx_sem)
-    to_smem.start()
-    to_smem.wait()
+    pump(2)
+
+    for s in range(2):
+        local = ids_v[:, s, :] - t * VOCAB_PART
+        local = jnp.where(jnp.logical_and(local >= 0, local < VOCAB_PART), local, ZERO_ROW)
+        for q in range(4):
+            ids_t[4 * s + q] = pltpu.roll(local, 128 - 24 * q, 1) if q else local
+
+    def to_smem(tp):
+        return pltpu.make_async_copy(ids_t.at[tp], ids_s.at[tp], idx_sem.at[tp])
+
+    for d in (2, 1, 3, 0):
+        for kk in (1 - k, k):
+            to_smem(2 * ((x + d) % 4) + kk).start()
+    keep_w.wait()
 
     first_half = lax.broadcasted_iota(jnp.int32, (16, 128), 1) < 64
 
     def look_up(tp, dst, n):
-        s = tp // 4
-        start = 24 * (tp % 4)
+        to_smem(tp).wait()
 
         @pl.loop(0, 32)
         def _(half):
             for m in range(2):
                 cc = 2 * half + m
                 for i in range(12):
-                    low[m, i:i + 1, :] = rows_ref[pl.ds(ids_s[cc, s, start + i], 1), :]
-                for i in range(12):
-                    high[m, i:i + 1, :] = rows_ref[pl.ds(ids_s[cc, s, start + 12 + i], 1), :]
+                    first = rows_ref[pl.ds(ids_s[tp, cc, i], 1), :]
+                    second = rows_ref[pl.ds(ids_s[tp, cc, 12 + i], 1), :]
+                    pairs[m, i:i + 1, :] = jnp.where(first_half[:1], first, second)
             for m in range(2):
-                dst[n, 2 * half + m] = jnp.where(first_half, low[m], high[m]).astype(jnp.bfloat16)
-
-    low[...] = jnp.zeros_like(low)
-    high[...] = jnp.zeros_like(high)
+                dst[n, 2 * half + m] = pairs[m].astype(jnp.bfloat16)
+
+    pairs[...] = jnp.zeros_like(pairs)
 
     def to_other(n):
         return remote(for_other.at[n], from_other.at[n], rs4_send.at[n], rs4_recv.at[n], other, c)
@@ -391,6 +455,8 @@
         xx = (x + d) % 4
         look_up(2 * xx + 1 - k, for_other, n)
         to_other(n).start()
+        if n < 2:
+            pump(3 + n)
         look_up(2 * xx + k, own, n)
         land(from_other.at[n], rs4_recv.at[n])
         own[n] = own[n] + from_other[n]
@@ -410,11 +476,14 @@
         send_rows(i).start()
 
     pieces[c] = summed[c]
+    pump(5)
 
     @pl.loop(1, 64)
     def _(i):
         src = (c + i) % 64
         land(pieces.at[src], a2a_recv.at[src])
+
+    pump(6)
 
     def add_squares(i, acc):
         piece = pieces[i].astype(jnp.float32)
@@ -464,12 +533,19 @@
     land(out_ref.at[across, 1], agr_recv.at[1])
     hand_across = hand_over(out_ref.at[across], across, 3)
     hand_across.start()
+    pump(7)
 
     flip = 1 - 2 * k
     land(out_ref.at[t + flip], agp_recv.at[0])
     land(out_ref.at[left + flip], agp_recv.at[1])
     land(out_ref.at[right + flip], agp_recv.at[2])
     land(out_ref.at[across + flip], agp_recv.at[3])
+
+    pump(8)
+    for stage in range(2):
+        for half, up in w_rings:
+            for step in range(4 if up else 3):
+                w_step(stage, half, up, step)[0]().wait_send()
 
     @pl.loop(1, 64)
     def _(i):
@@ -484,21 +560,21 @@
         copy.wait_send()
 
 
-def embed(ids, table, gain):
+def embed(ids, table, gain, w_part):
     vmem = pl.BlockSpec(memory_space=pltpu.VMEM)
     dma = pltpu.SemaphoreType.DMA
     slabs = (64, 16, 128)
     return pl.pallas_call(
         embed_kernel,
-        out_shape=jax.ShapeDtypeStruct((8, 2, 24, 2048), jnp.bfloat16),
-        in_specs=[vmem, vmem, vmem],
-        out_specs=vmem,
+        out_shape=(jax.ShapeDtypeStruct((8, 2, 24, 2048), jnp.bfloat16),
+                   jax.ShapeDtypeStruct((8, 8, 2, 32, 768), jnp.bfloat16)),
+        in_specs=[vmem, vmem, vmem, vmem],
+        out_specs=(vmem, pl.BlockSpec(memory_space=pl.ANY)),
         scratch_shapes=[
             pltpu.VMEM((VOCAB_PART // 128 * 128 + 128, 128), jnp.float32),
             pltpu.VMEM((64, 2, 128), jnp.int32),
-            pltpu.VMEM((64, 2, 128), jnp.int32),
-            pltpu.SMEM((64, 2, 128), jnp.int32),
-            pltpu.VMEM((2, 16, 128), jnp.float32),
+            pltpu.VMEM((8, 64, 128), jnp.int32),
+            pltpu.SMEM((8, 64, 128), jnp.int32),
             pltpu.VMEM((2, 16, 128), jnp.float32),
             pltpu.VMEM((4,) + slabs, jnp.bfloat16),
             pltpu.VMEM((4,) + slabs, jnp.bfloat16),
@@ -508,23 +584,24 @@
             pltpu.VMEM(slabs, jnp.bfloat16),
             pltpu.VMEM((24, 4096), jnp.float32),
             pltpu.VMEM((2, 24, 2048), jnp.bfloat16),
-            dma((64,)), dma((64,)), dma,
+            dma((64,)), dma((64,)), dma((8,)),
             dma((4,)), dma((4,)), dma((3,)), dma((3,)),
             dma((64,)), dma((64,)),
             dma((2,)), dma((2,)), dma((2,)), dma((2,)), dma((4,)), dma((4,)),
+            dma((2, 2, 7)), dma((2, 2, 7)), dma,
         ],
         compiler_params=pltpu.CompilerParams(
             collective_id=0, has_side_effects=True, vmem_limit_bytes=VMEM_LIMIT),
         name="look_up_scatter_norm",
-    )(ids, table, gain)
+    )(ids, table, gain, w_part)
 
 
 def shards(token_ids, embed_table, input_gain, w_qkv, q_gain, k_gain):
     context_rank = lax.axis_index("context")
     local_len = token_ids.shape[1]
-    w_all = lax.all_gather(w_qkv, "context", axis=0, tiled=True)
     ids = jnp.pad(token_ids, ((0, 0), (0, 128 - local_len)))
-    normed = embed(ids, embed_table, input_gain[None])
+    normed, w_all = embed(ids, embed_table, input_gain[None], w_qkv.reshape(2, 32, -1))
+    w_all = w_all.reshape(4096, -1)
     positions = context_rank * local_len + jnp.arange(local_len, dtype=jnp.int32)
     cos_t, sin_t = rope_tables(positions, HD)
     sin_t = jnp.concatenate([-sin_t[:, :64], sin_t[:, 64:]], axis=-1)

time: 177 us -> 155 us (0.88)
  the two profiles are of different devices: /device:TPU:63 before, /device:TPU:15 now
where the time goes in v3:
time: 155 us
  Pallas kernels  151 us (97%)
  local copies, waits for them, and re-layouts  2.88 us (2%)
  other arithmetic  1.75 us (1%)
    pallas_call x1, Pallas kernels, embed(): pl.pallas_call(embed_kernel, out_shape=(jax.ShapeDtypeStruct((8, 2, 24, 2...  87 us
    pallas_call x1, Pallas kernels, attention(): pl.pallas_call(attention_kernel, out_shape=jax.ShapeDtypeStruct((1, 768,...  63.6 us

profile of v3, /device:TPU:15, one launch (start us, length us, event | category | flops | bytes accessed | tf_op | source)
XLA Modules:
  0.0 155.2 jit_solution(7566732858309411621)
XLA Ops:
  0.0 1.3 pad.4.ids_ref
  1.3 0.1 broadcast_multiply_fusion
  1.4 0.9 fusion
  2.2 0.1 slice_negate_fusion
  2.3 0.7 pad_maximum_fusion.1.sin_ref
  3.0 87.0 %look_up_scatter_norm.1 = (bf16[8,2,24,2048]{3,2,1,0:T(8,128)(2,1)}, bf16[8,8,2,32,768]{4,3,2,1,0:T(8,128)(2,1)}) custom-call(s32[2,128]{1,0:T(2,128)} %pad.4.ids_ref, bf16[64,18992]{1,0:T(8,128)(2,1)} %table_ref.1, f32[1,4096]{1,0:T(1,128)} %bitcast.7, bf16[2,32,768]{2,1,0:T(8,128)(2,1)} %bitcast.6), custom_call_target="tpu_custom_call" | custom-call | tf_op jit(solution)/shard_map/look_up_scatter_norm/pallas_call | solution.py:567
  90.0 63.6 %project_exchange_attend.1 = bf16[1,768,128]{2,1,0:T(8,128)(2,1)} custom-call(bf16[8,2,24,2048]{3,2,1,0:T(8,128)(2,1)} %get-tuple-element.7.x_ref, bf16[4096,768]{1,0:T(8,128)(2,1)} %bitcast.5, f32[96,128]{1,0:T(8,128)} %get-tuple-element.12.cos_ref, f32[96,128]{1,0:T(8,128)} %pad_maximum_fusion.1.sin_ref, f32[1,128]{1,0:T(1,128)} %bitcast.8, f32[1,128]{1,0:T(1,128)} %bitcast.9), custom_call_target="tpu_custom_call" | custom-call | tf_op jit(solution)/shard_map/project_exchange_attend/pallas_call | solution.py:289
  153.6 1.6 %copy.8 = bf16[1,768,128]{2,1,0:T(8,128)(2,1)} copy(bf16[1,768,128]{2,1,0:T(8,128)(2,1)} %project_exchange_attend.1) | data formatting | bytes 393216
  (2 shorter events, 0.0 us)

commit v4 on v3

--- a/solution.py
+++ b/solution.py
@@ -42,6 +42,14 @@
     return own.astype(jnp.int32)
 
 
+def group_of(c):
+    return 8 * ((c // 8 + c % 8) % 8) + c % 8
+
+
+def holder_of(g):
+    return 8 * ((g // 8 - g % 8 + 8) % 8) + g % 8
+
+
 K0 = 8
 V0 = 72
 W_CHUNKS = 8
@@ -54,6 +62,7 @@
     t = lax.axis_index("tensor")
     c = lax.axis_index("context")
     x, k = t // 2, t % 2
+    g = group_of(c)
     chunk = w_buf.shape[1]
     w_copies = [
         pltpu.make_async_copy(w_hbm.at[pl.ds(i * chunk, chunk)], w_buf.at[i], w_sem.at[i])
@@ -68,10 +77,10 @@
     barrier = pltpu.get_barrier_semaphore()
     kept = jnp.int32(0)
     for i in range(8):
-        kept += greet(barrier, head_u // 6, 8 * t + i, t, c)
+        kept += greet(barrier, head_u // 6, holder_of(8 * t + i), t, c)
     for i in range(2):
-        kept += greet(barrier, (QH + group_u) // 6, 8 * t + 2 * y4 + i, t, c)
-        kept += greet(barrier, (QH + KVH + group_u) // 6, 8 * t + 2 * y4 + i, t, c)
+        kept += greet(barrier, (QH + group_u) // 6, holder_of(8 * t + 2 * y4 + i), t, c)
+        kept += greet(barrier, (QH + KVH + group_u) // 6, holder_of(8 * t + 2 * y4 + i), t, c)
     for d in range(1, 4):
         pl.semaphore_signal(barrier, inc=1, device_id=(t, c - y4 + (y4 + d) % 4), device_id_type=MESH)
     for d in range(1, 8):
@@ -107,10 +116,10 @@
         is_q = head < QH
         i = jnp.maximum(head - QH, 0)
         kind, group = i // KVH, i % KVH
-        to_c = s * QH + jnp.where(is_q, head, 4 * group + (c % 8) // 2)
-        to_t = c // 8
-        slot = jnp.where(is_q, c % 8, K0 + 64 * kind + c)
-        sem = jnp.where(is_q, c % 8, 8 + 2 * kind + c % 2)
+        to_c = s * QH + jnp.where(is_q, head, 4 * group + (g % 8) // 2)
+        to_t = g // 8
+        slot = jnp.where(is_q, g % 8, K0 + 64 * kind + g)
+        sem = jnp.where(is_q, g % 8, 8 + 2 * kind + g % 2)
         own = jnp.logical_and(to_t == t, to_c == c)
         far = remote(heads.at[b], blocks.at[slot], s1_send.at[b], s1_recv.at[sem], to_t, to_c)
 
@@ -132,10 +141,6 @@
     for b in range(12):
         stage1(b, True)
     base = 8 * t + 2 * y4
-    for i in range(2):
-        land(blocks.at[K0 + base + i], s1_recv.at[8 + i])
-        land(blocks.at[V0 + base + i], s1_recv.at[10 + i])
-
     def stage2(kind, d):
         first = (K0, V0)[kind] + base
         peer = (y4 + d) % 4
@@ -143,12 +148,10 @@
                       s2_send.at[kind, d], s2_recv.at[kind, y4], t, c - y4 + peer)
 
     for kind in range(2):
+        for i in range(2):
+            land(blocks.at[(K0, V0)[kind] + base + i], s1_recv.at[8 + 2 * kind + i])
         for d in range(1, 4):
             stage2(kind, d).start()
-    for kind in range(2):
-        for d in range(1, 4):
-            peer = (y4 + d) % 4
-            land(blocks.at[pl.ds((K0, V0)[kind] + 8 * t + 2 * peer, 2)], s2_recv.at[kind, peer])
 
     def slab(kind, tt):
         return blocks.at[pl.ds((K0, V0)[kind] + 8 * tt, 8)]
@@ -186,15 +189,20 @@
         2: [(0, 1), (1, 1), (0, 0), (1, 0)],
         3: [(1, 0), (0, 0), (0, 2), (1, 2), (0, 1), (1, 1)],
     }
-    for xx in range(4):
-        @pl.when(x == xx)
-        def _(xx=xx):
-            for n, (kind, of, to) in enumerate(own_list[xx]):
-                along_x(kind, of, to, n).start()
-            for kind in range(2):
+    for now in range(2):
+        for d in range(1, 4):
+            peer = (y4 + d) % 4
+            land(blocks.at[pl.ds((K0, V0)[now] + 8 * t + 2 * peer, 2)], s2_recv.at[now, peer])
+        for xx in range(4):
+            @pl.when(x == xx)
+            def _(xx=xx):
+                for n, (kind, of, to) in enumerate(own_list[xx]):
+                    if kind == now:
+                        along_x(kind, of, to, n).start()
+
                 @pl.when(k == 0)
                 def _():
-                    across(kind, xx).start()
+                    across(now, xx).start()
 
     score_scale = HD ** (-0.5)
     rows = 256
@@ -316,7 +324,7 @@
 
 
 def embed_kernel(ids_ref, table_ref, gain_ref, w_ref, out_ref, w_out,
-                 rows_ref, ids_v, ids_t, ids_s, pairs,
+                 rows_ref, id_row, ids_v, ids_t, ids_s, pairs,
                  for_other, own, from_other, from_x, summed, pieces, wide_ref, normed,
                  ids_send, ids_recv, idx_sem, rs4_send, rs4_recv, rsx_send, rsx_recv,
                  a2a_send, a2a_recv, agx_send, agx_recv, agr_send, agr_recv, agp_send, agp_recv,
@@ -337,9 +345,11 @@
     for d in range(1, 8):
         pl.semaphore_signal(barrier, inc=1, device_id=((t + d) % 8, c), device_id_type=MESH)
 
+    twice = (lax.broadcasted_iota(jnp.int32, (64, 128), 1) % 64
+             == lax.broadcasted_iota(jnp.int32, (64, 128), 0)).astype(jnp.float32).astype(jnp.bfloat16)
+
     def transpose(block):
-        wide = block.astype(jnp.float32)
-        return jnp.concatenate([wide, wide], axis=0).T
+        return lax.dot_general(block, twice, (((0,), (0,)), ((), ())), preferred_element_type=jnp.float32)
 
     full = VOCAB_PART // 128
 
@@ -349,14 +359,16 @@
             at = pl.multiple_of(b * 128, 128)
             rows_ref[pl.ds(at, 128), :] = transpose(table_ref[:, pl.ds(at, 128)])
 
-    turn(0, full // 2)
+    id_row[...] = jnp.zeros_like(id_row)
+    id_row[:, :ids_ref.shape[1]] = ids_ref[...]
+    turn(0, 50)
     pl.semaphore_wait(barrier, 70)
 
     def land(dst, sem):
         pltpu.make_async_copy(dst, dst, sem).wait()
 
     def send_ids(i):
-        return remote(ids_ref, ids_v.at[c], ids_send.at[i], ids_recv.at[c], t, (c + i) % 64)
+        return remote(id_row, ids_v.at[c], ids_send.at[i], ids_recv.at[c], t, (c + i) % 64)
 
     @pl.loop(1, 64)
     def _(i):
@@ -397,21 +409,23 @@
                         land(arriving, sem)
 
     pump(0)
-    ids_v[c] = ids_ref[...]
-    turn(full // 2, full)
+    ids_v[c] = id_row[...]
+    turn(50, 84)
+    pump(1)
+    turn(84, 116)
+    pump(2)
+    turn(116, full)
     rest = VOCAB_PART - full * 128
     tail = jnp.concatenate(
         [table_ref[:, full * 128:].astype(jnp.float32), jnp.zeros((64, 128 - rest), jnp.float32)], axis=1)
-    rows_ref[full * 128:, :] = transpose(tail)
-
-    pump(1)
+    rows_ref[full * 128:, :] = transpose(tail.astype(jnp.bfloat16))
+
+    pump(3)
 
     @pl.loop(1, 64)
     def _(i):
         src = (c + i) % 64
         land(ids_v.at[src], ids_recv.at[src])
-
-    pump(2)
 
     for s in range(2):
         local = ids_v[:, s, :] - t * VOCAB_PART
@@ -426,6 +440,7 @@
         for kk in (1 - k, k):
             to_smem(2 * ((x + d) % 4) + kk).start()
     keep_w.wait()
+    pump(4)
 
     first_half = lax.broadcasted_iota(jnp.int32, (16, 128), 1) < 64
 
@@ -455,8 +470,8 @@
         xx = (x + d) % 4
         look_up(2 * xx + 1 - k, for_other, n)
         to_other(n).start()
-        if n < 2:
-            pump(3 + n)
+        if n == 2:
+            pump(5)
         look_up(2 * xx + k, own, n)
         land(from_other.at[n], rs4_recv.at[n])
         own[n] = own[n] + from_other[n]
@@ -469,21 +484,21 @@
 
     def send_rows(i):
         peer = (c + i) % 64
-        return remote(summed.at[peer], pieces.at[c], a2a_send.at[i], a2a_recv.at[c], t, peer)
+        return remote(summed.at[group_of(peer)], pieces.at[c], a2a_send.at[i], a2a_recv.at[c], t, peer)
 
     @pl.loop(1, 64)
     def _(i):
         send_rows(i).start()
 
-    pieces[c] = summed[c]
-    pump(5)
+    pieces[c] = summed[group_of(c)]
+    pump(6)
 
     @pl.loop(1, 64)
     def _(i):
         src = (c + i) % 64
         land(pieces.at[src], a2a_recv.at[src])
 
-    pump(6)
+    pump(7)
 
     def add_squares(i, acc):
         piece = pieces[i].astype(jnp.float32)
@@ -533,7 +548,6 @@
     land(out_ref.at[across, 1], agr_recv.at[1])
     hand_across = hand_over(out_ref.at[across], across, 3)
     hand_across.start()
-    pump(7)
 
     flip = 1 - 2 * k
     land(out_ref.at[t + flip], agp_recv.at[0])
@@ -572,6 +586,7 @@
         out_specs=(vmem, pl.BlockSpec(memory_space=pl.ANY)),
         scratch_shapes=[
             pltpu.VMEM((VOCAB_PART // 128 * 128 + 128, 128), jnp.float32),
+            pltpu.VMEM((2, 128), jnp.int32),
             pltpu.VMEM((64, 2, 128), jnp.int32),
             pltpu.VMEM((8, 64, 128), jnp.int32),
             pltpu.SMEM((8, 64, 128), jnp.int32),
@@ -599,10 +614,9 @@
 def shards(token_ids, embed_table, input_gain, w_qkv, q_gain, k_gain):
     context_rank = lax.axis_index("context")
     local_len = token_ids.shape[1]
-    ids = jnp.pad(token_ids, ((0, 0), (0, 128 - local_len)))
-    normed, w_all = embed(ids, embed_table, input_gain[None], w_qkv.reshape(2, 32, -1))
+    normed, w_all = embed(token_ids, embed_table, input_gain[None], w_qkv.reshape(2, 32, -1))
     w_all = w_all.reshape(4096, -1)
-    positions = context_rank * local_len + jnp.arange(local_len, dtype=jnp.int32)
+    positions = group_of(context_rank) * local_len + jnp.arange(local_len, dtype=jnp.int32)
     cos_t, sin_t = rope_tables(positions, HD)
     sin_t = jnp.concatenate([-sin_t[:, :64], sin_t[:, 64:]], axis=-1)
     return attention(normed, w_all, cos_t, sin_t, q_gain[None], k_gain[None])

time: 155 us -> 148 us (0.955)
  the two profiles are of different devices: /device:TPU:15 before, /device:TPU:127 now
where the time goes in v4:
time: 148 us
  Pallas kernels  145 us (98%)
  other arithmetic  1.76 us (1%)
  local copies, waits for them, and re-layouts  1.62 us (1%)
    pallas_call x1, Pallas kernels, embed(): pl.pallas_call(embed_kernel, out_shape=(jax.ShapeDtypeStruct((8, 2, 24, 2...  82.7 us
    pallas_call x1, Pallas kernels, attention(): pl.pallas_call(attention_kernel, out_shape=jax.ShapeDtypeStruct((1, 768,...  62.1 us

profile of v4, /device:TPU:127, one launch (start us, length us, event | category | flops | bytes accessed | tf_op | source)
XLA Modules:
  0.0 148.2 jit_solution(1480210157072939340)
XLA Ops:
  0.0 0.1 broadcast_multiply_fusion
  0.1 0.9 fusion
  1.0 0.1 slice_negate_fusion
  1.1 0.7 pad_maximum_fusion.1.sin_ref
  1.8 82.7 %look_up_scatter_norm.1 = (bf16[8,2,24,2048]{3,2,1,0:T(8,128)(2,1)}, bf16[8,8,2,32,768]{4,3,2,1,0:T(8,128)(2,1)}) custom-call(s32[2,96]{1,0:T(2,128)} %ids_ref.1, bf16[64,18992]{1,0:T(8,128)(2,1)} %table_ref.1, f32[1,4096]{1,0:T(1,128)} %bitcast.7, bf16[2,32,768]{2,1,0:T(8,128)(2,1)} %bitcast.6), custom_call_target="tpu_custom_call" | custom-call | tf_op jit(solution)/shard_map/look_up_scatter_norm/pallas_call | solution.py:581
  84.5 62.1 %project_exchange_attend.1 = bf16[1,768,128]{2,1,0:T(8,128)(2,1)} custom-call(bf16[8,2,24,2048]{3,2,1,0:T(8,128)(2,1)} %get-tuple-element.7.x_ref, bf16[4096,768]{1,0:T(8,128)(2,1)} %bitcast.5, f32[96,128]{1,0:T(8,128)} %get-tuple-element.12.cos_ref, f32[96,128]{1,0:T(8,128)} %pad_maximum_fusion.1.sin_ref, f32[1,128]{1,0:T(1,128)} %bitcast.8, f32[1,128]{1,0:T(1,128)} %bitcast.9), custom_call_target="tpu_custom_call" | custom-call | tf_op jit(solution)/shard_map/project_exchange_attend/pallas_call | solution.py:297
  146.6 1.6 %copy.8 = bf16[1,768,128]{2,1,0:T(8,128)(2,1)} copy(bf16[1,768,128]{2,1,0:T(8,128)(2,1)} %project_exchange_attend.1) | data formatting | bytes 393216
  (2 shorter events, 0.0 us)

commit v5 on v4

--- a/solution.py
+++ b/solution.py
@@ -205,7 +205,7 @@
                     across(now, xx).start()
 
     score_scale = HD ** (-0.5)
-    rows = 256
+    rows = 384
 
     def update(state, q, keys, vals, mask):
         old_max, old_total, old_acc = state
@@ -223,7 +223,7 @@
 
     for i in range(8):
         land(blocks.at[i], s1_recv.at[i])
-    for i in range(3):
+    for i in range(2):
         q = blocks[0:8].reshape(768, HD)[rows * i:rows * (i + 1)]
         width = rows * (i + 1)
         keys = blocks[pl.ds(K0 + 8 * t, 8)].reshape(768, HD)[:width]
@@ -260,7 +260,7 @@
                     arrived_x(kind, of)
                     across(kind, of).start()
 
-    for i in range(3):
+    for i in range(2):
         max_ref[i], total_ref[i], sum_ref[i] = attend(i, k, x)
 
     for of in range(4):
@@ -269,7 +269,7 @@
             def _():
                 land(slab(kind, 2 * of + 1 - k), s4_recv.at[kind, of])
 
-    for i in range(3):
+    for i in range(2):
         _, total, acc = attend(i, 1 - k, x + k)
         o_ref[0, rows * i:rows * (i + 1), :] = (acc / total).astype(jnp.bfloat16)
 
@@ -309,9 +309,9 @@
             dma((2, 4)), dma((2, 4)),
             dma((6,)), dma((2, 4)),
             dma((2, 4)), dma((2, 4)),
-            pltpu.VMEM((3, 256, 1), jnp.float32),
-            pltpu.VMEM((3, 256, 1), jnp.float32),
-            pltpu.VMEM((3, 256, HD), jnp.float32),
+            pltpu.VMEM((2, 384, 1), jnp.float32),
+            pltpu.VMEM((2, 384, 1), jnp.float32),
+            pltpu.VMEM((2, 384, HD), jnp.float32),
         ],
         compiler_params=pltpu.CompilerParams(
             collective_id=1, has_side_effects=True, vmem_limit_bytes=VMEM_LIMIT),
@@ -386,12 +386,17 @@
         to = (here + sign) % 8
         peer = 8 * z + to if (stage == 0) == (half == 0) else 8 * to + y
         n = step if up else 4 + step
+        arriving = w_block(stage, half, (here - sign * (step + 1)) % 8)
+        if step == 3:
+            size = (16, 4)[stage]
+            part = pl.ds(0 if up else size, size)
+            block, arriving = block.at[part], arriving.at[part]
 
         def copy():
             return remote(w_ref.at[half] if (stage, step) == (0, 0) else block, block,
                           w_send.at[stage, half, n], w_recv.at[stage, half, n], t, peer)
 
-        return copy, w_block(stage, half, (here - sign * (step + 1)) % 8), w_recv.at[stage, half, n]
+        return copy, arriving, w_recv.at[stage, half, n]
 
     w_rings = [(half, up) for half in range(2) for up in (True, False)]
 
@@ -401,12 +406,11 @@
             if not 0 <= stage < 2:
                 continue
             for half, up in w_rings:
-                if at < (4 if up else 3):
-                    copy, arriving, sem = w_step(stage, half, up, at)
-                    if starting:
-                        copy().start()
-                    else:
-                        land(arriving, sem)
+                copy, arriving, sem = w_step(stage, half, up, at)
+                if starting:
+                    copy().start()
+                else:
+                    land(arriving, sem)
 
     pump(0)
     ids_v[c] = id_row[...]
@@ -470,14 +474,13 @@
         xx = (x + d) % 4
         look_up(2 * xx + 1 - k, for_other, n)
         to_other(n).start()
-        if n == 2:
-            pump(5)
         look_up(2 * xx + k, own, n)
         land(from_other.at[n], rs4_recv.at[n])
         own[n] = own[n] + from_other[n]
         if d:
             to_chip(n, xx).start()
 
+    pump(5)
     for n in range(3):
         land(from_x.at[n], rsx_recv.at[n])
     summed[...] = (own[3] + from_x[0]) + (from_x[1] + from_x[2])
@@ -558,7 +561,7 @@
     pump(8)
     for stage in range(2):
         for half, up in w_rings:
-            for step in range(4 if up else 3):
+            for step in range(4):
                 w_step(stage, half, up, step)[0]().wait_send()
 
     @pl.loop(1, 64)
@@ -603,7 +606,7 @@
             dma((4,)), dma((4,)), dma((3,)), dma((3,)),
             dma((64,)), dma((64,)),
             dma((2,)), dma((2,)), dma((2,)), dma((2,)), dma((4,)), dma((4,)),
-            dma((2, 2, 7)), dma((2, 2, 7)), dma,
+            dma((2, 2, 8)), dma((2, 2, 8)), dma,
         ],
         compiler_params=pltpu.CompilerParams(
             collective_id=0, has_side_effects=True, vmem_limit_bytes=VMEM_LIMIT),

time: 148 us -> 149 us (level)
  the two profiles are of different devices: /device:TPU:127 before, /device:TPU:143 now
where the time goes in v5:
time: 149 us; the launch traced here: 148 us
  Pallas kernels  145 us (97%)
  other arithmetic  1.76 us (1%)
  local copies, waits for them, and re-layouts  1.62 us (1%)
    pallas_call x1, Pallas kernels, embed(): pl.pallas_call(embed_kernel, out_shape=(jax.ShapeDtypeStruct((8, 2, 24, 2...  87 us
    pallas_call x1, Pallas kernels, attention(): pl.pallas_call(attention_kernel, out_shape=jax.ShapeDtypeStruct((1, 768,...  57.9 us

profile of v5, /device:TPU:143, one launch (start us, length us, event | category | flops | bytes accessed | tf_op | source)
XLA Modules:
  0.0 148.3 jit_solution(4183037149198784498)
XLA Ops:
  0.0 0.1 broadcast_multiply_fusion
  0.1 0.9 fusion
  1.0 0.1 slice_negate_fusion
  1.1 0.7 pad_maximum_fusion.1.sin_ref
  1.8 87.0 %look_up_scatter_norm.1 = (bf16[8,2,24,2048]{3,2,1,0:T(8,128)(2,1)}, bf16[8,8,2,32,768]{4,3,2,1,0:T(8,128)(2,1)}) custom-call(s32[2,96]{1,0:T(2,128)} %ids_ref.1, bf16[64,18992]{1,0:T(8,128)(2,1)} %table_ref.1, f32[1,4096]{1,0:T(1,128)} %bitcast.7, bf16[2,32,768]{2,1,0:T(8,128)(2,1)} %bitcast.6), custom_call_target="tpu_custom_call" | custom-call | tf_op jit(solution)/shard_map/look_up_scatter_norm/pallas_call | solution.py:584
  88.8 57.9 %project_exchange_attend.1 = bf16[1,768,128]{2,1,0:T(8,128)(2,1)} custom-call(bf16[8,2,24,2048]{3,2,1,0:T(8,128)(2,1)} %get-tuple-element.7.x_ref, bf16[4096,768]{1,0:T(8,128)(2,1)} %bitcast.5, f32[96,128]{1,0:T(8,128)} %get-tuple-element.12.cos_ref, f32[96,128]{1,0:T(8,128)} %pad_maximum_fusion.1.sin_ref, f32[1,128]{1,0:T(1,128)} %bitcast.8, f32[1,128]{1,0:T(1,128)} %bitcast.9), custom_call_target="tpu_custom_call" | custom-call | tf_op jit(solution)/shard_map/project_exchange_attend/pallas_call | solution.py:297
  146.7 1.6 %copy.8 = bf16[1,768,128]{2,1,0:T(8,128)(2,1)} copy(bf16[1,768,128]{2,1,0:T(8,128)(2,1)} %project_exchange_attend.1) | data formatting | bytes 393216
  (2 shorter events, 0.0 us)

commit v6 on v5

--- a/solution.py
+++ b/solution.py
@@ -474,13 +474,15 @@
         xx = (x + d) % 4
         look_up(2 * xx + 1 - k, for_other, n)
         to_other(n).start()
+        if n == 2:
+            pump(5)
         look_up(2 * xx + k, own, n)
         land(from_other.at[n], rs4_recv.at[n])
         own[n] = own[n] + from_other[n]
         if d:
             to_chip(n, xx).start()
 
-    pump(5)
+    pump(6)
     for n in range(3):
         land(from_x.at[n], rsx_recv.at[n])
     summed[...] = (own[3] + from_x[0]) + (from_x[1] + from_x[2])
@@ -494,14 +496,12 @@
         send_rows(i).start()
 
     pieces[c] = summed[group_of(c)]
-    pump(6)
+    pump(7)
 
     @pl.loop(1, 64)
     def _(i):
         src = (c + i) % 64
         land(pieces.at[src], a2a_recv.at[src])
-
-    pump(7)
 
     def add_squares(i, acc):
         piece = pieces[i].astype(jnp.float32)

time: 149 us -> 149 us (level)
  the two profiles are of different devices: /device:TPU:143 before, /device:TPU:255 now
where the time goes in v6:
time: 149 us; the launch traced here: 148 us
  Pallas kernels  145 us (97%)
  other arithmetic  1.76 us (1%)
  local copies, waits for them, and re-layouts  1.62 us (1%)
    pallas_call x1, Pallas kernels, embed(): pl.pallas_call(embed_kernel, out_shape=(jax.ShapeDtypeStruct((8, 2, 24, 2...  85.2 us
    pallas_call x1, Pallas kernels, attention(): pl.pallas_call(attention_kernel, out_shape=jax.ShapeDtypeStruct((1, 768,...  59.7 us

profile of v6, /device:TPU:255, one launch (start us, length us, event | category | flops | bytes accessed | tf_op | source)
XLA Modules:
  0.0 148.4 jit_solution(11813259743392195699)
XLA Ops:
  0.0 0.1 broadcast_multiply_fusion
  0.1 0.9 fusion
  1.0 0.1 slice_negate_fusion
  1.1 0.7 pad_maximum_fusion.1.sin_ref
  1.8 85.2 %look_up_scatter_norm.1 = (bf16[8,2,24,2048]{3,2,1,0:T(8,128)(2,1)}, bf16[8,8,2,32,768]{4,3,2,1,0:T(8,128)(2,1)}) custom-call(s32[2,96]{1,0:T(2,128)} %ids_ref.1, bf16[64,18992]{1,0:T(8,128)(2,1)} %table_ref.1, f32[1,4096]{1,0:T(1,128)} %bitcast.7, bf16[2,32,768]{2,1,0:T(8,128)(2,1)} %bitcast.6), custom_call_target="tpu_custom_call" | custom-call | tf_op jit(solution)/shard_map/look_up_scatter_norm/pallas_call | solution.py:584
  87.0 59.7 %project_exchange_attend.1 = bf16[1,768,128]{2,1,0:T(8,128)(2,1)} custom-call(bf16[8,2,24,2048]{3,2,1,0:T(8,128)(2,1)} %get-tuple-element.7.x_ref, bf16[4096,768]{1,0:T(8,128)(2,1)} %bitcast.5, f32[96,128]{1,0:T(8,128)} %get-tuple-element.12.cos_ref, f32[96,128]{1,0:T(8,128)} %pad_maximum_fusion.1.sin_ref, f32[1,128]{1,0:T(1,128)} %bitcast.8, f32[1,128]{1,0:T(1,128)} %bitcast.9), custom_call_target="tpu_custom_call" | custom-call | tf_op jit(solution)/shard_map/project_exchange_attend/pallas_call | solution.py:297
  146.7 1.6 %copy.8 = bf16[1,768,128]{2,1,0:T(8,128)(2,1)} copy(bf16[1,768,128]{2,1,0:T(8,128)(2,1)} %project_exchange_attend.1) | data formatting | bytes 393216
  (2 shorter events, 0.0 us)
